TPU v7x, 256 devices: a whole 4x4x8 slice. The times are simulated.
256 devices in a mesh: dp: 4 (over x), expert: 16 (over z, core), tp: 4 (over y).
Axes of the slice: x: 4, y: 4, z: 8, core: 2. Of those that a mesh axis runs over, the one named last changes fastest.
Arguments:
- hidden: bfloat16 [16, 64, 96, 5632], P('expert', 'dp', None, 'tp'), parts along dimension 1, may hold values from -6 to 6
- down_weight: bfloat16 [16, 5632, 3072], P('expert', 'tp'), may hold values from -0.078125 to 0.078125
- routes: int32 [16384, 4], P(('dp', 'expert')), parts along dimension 0, may hold values from 0 to 15, all different within a row; in each aligned block of 256 rows (0 to 255, 256 to 511, ...) at most 96 rows name the same one
- route_weight: float32 [16384, 4], P(('dp', 'expert')), parts along dimension 0, may hold values from 0.05 to 1
- residual: bfloat16 [16384, 3072], P(('dp', 'expert'), 'tp'), parts along dimension 0, may hold values from -6 to 6
Outputs:
- mixed: bfloat16 [16384, 3072], P(('dp', 'expert'), 'tp'), parts along dimension 0
There are 4 independent parts, one for each index of `dp`. A program takes and returns all parts, laid end to end along the dimension named above; an argument that names none is the same for every part. Nothing has to cross between parts.
Inputs may be any that keep to these rules, and one draw needn't show every extreme that they name: `routes`: each row names 4 different experts. Among the 256 rows of one source group no expert is named by more than 96 rows, a bound that some of them reach.
All inputs are finite; a program needn't handle non-finite values.
Results may differ from a plain program's by a relative error of at most 0.0095.
Values may be sent and summed in bfloat16 or wider, within the bound.
A program may use at most 128 MiB of HBM per device.

v0:
```python
import jax
import jax.numpy as jnp
from jax import lax
from jax.sharding import PartitionSpec as P

EXPERTS = 16


def slot_table(routes):
    expert_ids = jnp.arange(EXPERTS, dtype=jnp.int32)
    matches = (routes[:, :, None] == expert_ids[None, None, :]).astype(jnp.int32)
    onehot = jnp.sum(matches, axis=1)
    before = jnp.cumsum(onehot, axis=0) - onehot
    return jnp.sum(matches * before[:, None, :], axis=2)


def combine(received, routes, route_weight, slot_of):
    capacity = received.shape[1]
    width = received.shape[2]
    flattened = received.reshape(-1, width)
    slot_index = (routes * capacity + slot_of).reshape(-1)
    picked = (
        flattened[slot_index].astype(jnp.float32).reshape(routes.shape[0], routes.shape[1], width)
    )
    share = route_weight / jnp.sum(route_weight, axis=1, keepdims=True)
    return jnp.sum(share[:, :, None] * picked, axis=1)


def on_device(hidden, down_weight, routes, route_weight, residual):
    slot_of = slot_table(routes)
    partial_value = jnp.einsum(
        "lsch,lhd->slcd", hidden, down_weight, preferred_element_type=jnp.float32
    ).astype(jnp.bfloat16)
    received = lax.all_to_all(partial_value, "expert", split_axis=0, concat_axis=1, tiled=True)
    mixed_part = combine(received[0], routes, route_weight, slot_of)
    expert_mix = lax.psum_scatter(
        mixed_part.astype(jnp.bfloat16), "tp", scatter_dimension=1, tiled=True
    ).astype(jnp.float32)
    return (residual.astype(jnp.float32) + expert_mix).astype(jnp.bfloat16)


def solution(mesh):
    return jax.shard_map(
        on_device,
        mesh=mesh,
        in_specs=(
            P("expert", "dp", None, "tp"),
            P("expert", "tp", None),
            P(("dp", "expert"), None),
            P(("dp", "expert"), None),
            P(("dp", "expert"), "tp"),
        ),
        out_specs=P(("dp", "expert"), "tp"),
        check_vma=False,
    )
```

profile of v0, /device:TPU:1, one launch (start us, length us, event | category | flops | bytes accessed | tf_op | source)
XLA Modules:
  0.0 319.8 jit_solution(6353277664045412335)
XLA Ops:
  6.5 20.0 %convert_bitcast_fusion = bf16[16,1,96,3072]{3,2,1,0:T(8,128)(2,1)} fusion(bf16[1,1408,3072]{2,1,0:T(8,128)(2,1)} %param.6, bf16[1,16,96,1408]{3,2,1,0:T(8,128)(2,1)} %param.5), kind=kOutput, calls=%fused_computation.2 | convolution fusion | flops 13292273664 | bytes 22413312 | tf_op jit(solution)/shard_map/lsch,lhd->slcd/dot_general | solution.py:31
  26.5 0.0 copy-start.1
  26.5 0.0 copy-start.2
  26.5 10.1 %all-to-all-start = ((bf16[16,1,96,3072]{3,2,1,0:T(8,128)(2,1)}), bf16[16,1,96,3072]{3,2,1,0:T(8,128)(2,1)}, u32[]{:S(2)}, u32[]{:S(2)}) async-start(bf16[16,1,96,3072]{3,2,1,0:T(8,128)(2,1)} %convert_bitcast_fusion), calls=%async_computation | async-start | bytes 18874368 | tf_op jit(solution)/shard_map/all_to_all | solution.py:34
  36.6 0.0 reduce-scatter.2.cloned.1.call-start
  36.7 0.0 copy-done.1
  36.7 0.6 reduce-window.6
  37.3 0.2 slice_reduce_fusion
  37.5 0.1 fusion.5
  37.6 0.1 copy.25
  37.8 0.1 reshape.65
  37.9 0.0 copy-done.2
  37.9 0.1 copy.21
  38.1 204.4 %all-to-all-done = bf16[16,1,96,3072]{3,2,1,0:T(8,128)(2,1)} async-done(((bf16[16,1,96,3072]{3,2,1,0:T(8,128)(2,1)}), bf16[16,1,96,3072]{3,2,1,0:T(8,128)(2,1)}, u32[]{:S(2)}, u32[]{:S(2)}) %all-to-all-start) | async-done | bytes 9437216 | tf_op jit(solution)/shard_map/all_to_all | solution.py:34
  242.5 17.1 %gather_fusion = bf16[1024,3072]{1,0:T(8,128)(2,1)} fusion(bf16[1536,3072]{1,0:T(8,128)(2,1)} %bitcast.6, s32[1024]{0:T(1024)S(1)} %broadcast_clamp_fusion), kind=kCustom, calls=%fused_computation | custom fusion | bytes 12587008 | tf_op jit(solution)/shard_map/gather | solution.py:23
  259.6 12.2 %reshape.66 = f32[256,4,3072]{2,1,0:T(4,128)} reshape(bf16[1024,3072]{1,0:T(8,128)(2,1)} %gather_fusion) | data formatting | bytes 18874368 | tf_op jit(solution)/shard_map/convert_element_type | solution.py:23
  271.9 0.0 copy-start
  271.9 12.2 %multiply_reduce_fusion = bf16[256,3072]{1,0:T(8,128)(2,1)} fusion(f32[256,4,3072]{2,1,0:T(4,128)} %reshape.66, f32[256,4]{1,0:T(8,128)S(1)} %copy.21), kind=kLoop, calls=%fused_computation.1 | loop fusion | flops 5505024 | bytes 14159872 | tf_op jit(solution)/shard_map/reduce_sum | solution.py:26
  284.1 0.0 reduce-scatter.2.cloned.1.call-update
  284.1 27.0 %reduce-scatter.2.cloned.1.call-done = bf16[256,768]{1,0:T(8,128)(2,1)} async-done(((bf16[256,3072]{1,0:T(8,128)(2,1)}), bf16[256,768]{1,0:T(8,128)(2,1)}) %reduce-scatter.2.cloned.1.call-update) | async-done | bytes 393232 | tf_op jit(solution)/shard_map/reduce_scatter | solution.py:36
  311.1 0.0 copy-done
  311.1 1.8 add_convert_fusion
  (10 shorter events, 0.1 us)
Async XLA Ops:
  26.5 10.2 %copy-start.1 = (s32[256,4]{0,1:T(4,128)S(1)}, s32[256,4]{0,1:T(4,128)}, u32[]{:S(2)}) copy-start(s32[256,4]{0,1:T(4,128)} %param.7) | copy-start | bytes 12292
  26.5 11.4 %copy-start.2 = (f32[256,4]{0,1:T(4,128)S(1)}, f32[256,4]{0,1:T(4,128)}, u32[]{:S(2)}) copy-start(f32[256,4]{0,1:T(4,128)} %param.8) | copy-start | bytes 12292
  26.5 216.0 %all-to-all-start = ((bf16[16,1,96,3072]{3,2,1,0:T(8,128)(2,1)}), bf16[16,1,96,3072]{3,2,1,0:T(8,128)(2,1)}, u32[]{:S(2)}, u32[]{:S(2)}) async-start(bf16[16,1,96,3072]{3,2,1,0:T(8,128)(2,1)} %convert_bitcast_fusion), calls=%async_computation | async-start | bytes 18874368 | tf_op jit(solution)/shard_map/all_to_all | solution.py:34
  36.6 274.5 %reduce-scatter.2.cloned.1.call-start = ((), (), s32[]{:S(2)}) async-start(), calls=%async_computation.2 | async-start | bytes 1966080 | tf_op jit(solution)/shard_map/reduce_scatter | solution.py:36
  271.9 39.2 %copy-start = (bf16[256,768]{1,0:T(8,128)(2,1)S(1)}, bf16[256,768]{1,0:T(8,128)(2,1)}, u32[]{:S(2)}) copy-start(bf16[256,768]{1,0:T(8,128)(2,1)} %param.9) | copy-start | bytes 1179652
Sparse Core Ops, SparseCore 0:
  284.3 26.7 reduce-scatter.1
where the time goes:
time: 320 us
  waiting for transfers between devices  231 us (72%)
  local copies, waits for them, and re-layouts  30 us (9%)
  matrix products  20 us (6%)
  other arithmetic  14.9 us (5%)
  between operations  13.5 us (4%)
  starting transfers between devices  10.2 us (3%)
    all_to_all x1, waiting for transfers between devices, on_device(): lax.all_to_all(partial_value, 'expert', split_axis=0, concat_axis=1, tile...  204 us
    reduce_scatter x1, waiting for transfers between devices, on_device(): lax.psum_scatter(mixed_part.astype(jnp.bfloat16), 'tp', scatter_dimension...  27 us
    dot_general x1, matrix products, on_device(): jnp.einsum('lsch,lhd->slcd', hidden, down_weight, preferred_element_type=...  20 us
    gather x1, local copies, waits for them, and re-layouts, combine(): flattened[slot_index].astype(jnp.float32)  17.1 us
    reduce_sum x1, other arithmetic, combine(): return jnp.sum(share[:, :, None] * picked, axis=1)  12.2 us
    convert_element_type x1, local copies, waits for them, and re-layouts, combine(): flattened[slot_index].astype(jnp.float32)  12.2 us
    all_to_all x1, starting transfers between devices, on_device(): lax.all_to_all(partial_value, 'expert', split_axis=0, concat_axis=1, tile...  10.1 us
  transfers between devices with their start and end apart: 2, of which 2 were waited for; matrix products, arithmetic and copies ran while one was open for 0% of the time, Pallas kernels for 0%

commit v1 on v0

v1 whole, which is shorter than its diff:
```python
import functools

import jax
import jax.numpy as jnp
from jax import lax
from jax.experimental import pallas as pl
from jax.experimental.pallas import tpu as pltpu
from jax.sharding import PartitionSpec as P

MESH = pl.DeviceIdType.MESH

ORDER = (
    (4, 0), (4, 1), (3, 0), (-3, 0), (3, 1), (-3, 1), (2, 0), (-2, 0),
    (2, 1), (-2, 1), (1, 0), (-1, 0), (1, 1), (-1, 1), (0, 0), (0, 1),
)
PAIRS = len(ORDER) // 2
SLICE_SHIFT = (3, 1, 2, 0)
HOPS = ((0, 2, 1, 3), (1, 2, 0, 3))
COLUMN_TILE = 256


def kernel(
    hidden, weight, routes, route_weight, residual, out,
    w_buf, h_buf, part, ring_in, mixed_in, pick_hi, pick_lo,
    w_sem, h_sem, ring_send, ring_recv, z_send, z_recv,
):
    expert, tp = lax.axis_index("expert"), lax.axis_index("tp")
    n_tp = len(SLICE_SHIFT)
    cap, width = part.shape[2], part.shape[3]
    tokens, top = routes.shape
    chips = len(ORDER) // 2
    z, core = expert // 2, expert % 2
    up, down = lax.rem(tp + 1, n_tp), lax.rem(tp + n_tp - 1, n_tp)

    def place(shift, other):
        chip = lax.rem(z + (shift + chips), chips)
        return 2 * chip + (core if other == 0 else 1 - core)

    targets = [place(shift, other) for shift, other in ORDER]
    senders = [place(-shift, other) for shift, other in ORDER]

    barrier = pltpu.get_barrier_semaphore()
    for peer in (up, down):
        pl.semaphore_signal(barrier, inc=1, device_id={"tp": peer}, device_id_type=MESH)
    for k, (shift, other) in enumerate(ORDER):
        if (shift, other) != (0, 0):
            pl.semaphore_signal(barrier, inc=1, device_id={"expert": targets[k]}, device_id_type=MESH)

    def w_load(r):
        start = pl.multiple_of(lax.rem(tp + SLICE_SHIFT[r], n_tp) * width, width)
        return pltpu.make_async_copy(weight.at[0, :, pl.ds(start, width)], w_buf.at[r], w_sem.at[r])

    def h_load(k):
        return pltpu.make_async_copy(hidden.at[0, targets[k]], h_buf.at[k], h_sem.at[k])

    h_load(0).start()
    h_load(1).start()
    for r in range(n_tp):
        w_load(r).start()
    for k in range(2, len(ORDER)):
        h_load(k).start()

    lane = lax.broadcasted_iota(jnp.int32, (8, len(ORDER)), 1)
    ids = jnp.zeros((8, len(ORDER)), jnp.int32)
    for k in range(len(ORDER)):
        ids = jnp.where(lane == k, senders[k], ids)
    ids = jnp.broadcast_to(ids[0:1, :], (tokens, len(ORDER)))
    scores = route_weight[...]
    share = scores / jnp.sum(scores, axis=1, keepdims=True)
    chosen = routes[...]
    member = jnp.zeros((tokens, len(ORDER)), jnp.float32)
    portion = jnp.zeros((tokens, len(ORDER)), jnp.float32)
    for c in range(top):
        same = chosen[:, c : c + 1] == ids
        member = member + jnp.where(same, 1.0, 0.0)
        portion = portion + jnp.where(same, share[:, c : c + 1], 0.0)
    rows = lax.broadcasted_iota(jnp.int32, (tokens, tokens), 0)
    cols = lax.broadcasted_iota(jnp.int32, (tokens, tokens), 1)
    earlier = jnp.where(cols < rows, 1.0, 0.0).astype(jnp.bfloat16)
    before = jnp.dot(earlier, member.astype(jnp.bfloat16), preferred_element_type=jnp.float32)
    slot = jnp.where(member > 0.5, before.astype(jnp.int32), -len(ORDER) * cap)
    portion_hi = portion.astype(jnp.bfloat16).astype(jnp.float32)
    portion_lo = portion - portion_hi
    groups = pick_hi.shape[0]
    per_group = len(ORDER) // groups
    column = lax.broadcasted_iota(jnp.int32, (tokens, per_group * cap), 1)
    for g in range(groups):
        hi = jnp.zeros((tokens, per_group * cap), jnp.float32)
        lo = jnp.zeros((tokens, per_group * cap), jnp.float32)
        for q in range(per_group):
            k = g * per_group + q
            hit = column == slot[:, k : k + 1] + q * cap
            hi = jnp.where(hit, portion_hi[:, k : k + 1], hi)
            lo = jnp.where(hit, portion_lo[:, k : k + 1], lo)
        pick_hi[g] = hi.astype(jnp.bfloat16)
        pick_lo[g] = lo.astype(jnp.bfloat16)

    def ring_copy(i, way, hop):
        k = 2 * i + way
        return pltpu.make_async_remote_copy(
            src_ref=part.at[k, HOPS[way][hop]],
            dst_ref=ring_in.at[hop, k],
            send_sem=ring_send.at[hop, k],
            recv_sem=ring_recv.at[hop, k],
            device_id={"tp": (up, down)[way]},
            device_id_type=MESH,
        )

    def z_copy(k, target):
        return pltpu.make_async_remote_copy(
            src_ref=part.at[k, n_tp - 1],
            dst_ref=mixed_in.at[k],
            send_sem=z_send.at[k],
            recv_sem=z_recv.at[k],
            device_id={"expert": target},
            device_id_type=MESH,
        )

    def matmul(i, r):
        left = h_buf[pl.ds(2 * i, 2)].reshape(2 * cap, h_buf.shape[2])

        def tile(t, carry):
            at = pl.ds(pl.multiple_of(t * COLUMN_TILE, COLUMN_TILE), COLUMN_TILE)
            product = jnp.dot(left, w_buf[r, :, at], preferred_element_type=jnp.float32)
            part[pl.ds(2 * i, 2), r, :, at] = product.astype(jnp.bfloat16).reshape(2, cap, COLUMN_TILE)
            return carry

        lax.fori_loop(0, width // COLUMN_TILE, tile, 0)

    def arrive(i, hop):
        for way in range(2):
            ring_copy(i, way, hop).wait_recv()
        for way in range(2):
            k, r = 2 * i + way, HOPS[way][hop + 1]
            part[k, r] = part[k, r] + ring_in[hop, k]

    def step(n, carry):
        @pl.when(n < PAIRS)
        def _():
            for way in range(2):
                h = 2 * n + way
                pltpu.make_async_copy(hidden.at[0, 0], h_buf.at[h], h_sem.at[h]).wait()
            for r in range(n_tp):
                @pl.when(n == 0)
                def _():
                    w_load(r).wait()
                matmul(n, r)
                if r == 1:
                    @pl.when(n == 0)
                    def _():
                        pl.semaphore_wait(barrier, len(ORDER) + 1)
                    ring_copy(n, 0, 0).start()
                if r == 2:
                    ring_copy(n, 1, 0).start()

        for hop in range(2):
            i = n - 1 - hop

            @pl.when((i >= 0) & (i < PAIRS))
            def _():
                arrive(i, hop)
                for way in range(2):
                    ring_copy(i, way, hop + 1).start()

        i = n - 3

        @pl.when((i >= 0) & (i < PAIRS - 1))
        def _():
            arrive(i, 2)
            for way in range(2):
                shift = jnp.where(i == 0, 4, 3 - (i - 1) // 2)
                other = jnp.where(i == 0, way, lax.rem(i - 1, 2))
                chip = lax.rem(z + chips + (shift if way == 0 else -shift), chips)
                place_core = jnp.where(other == 0, core, 1 - core)
                z_copy(2 * i + way, 2 * chip + place_core).start()

        return carry

    lax.fori_loop(0, PAIRS + 2, step, 0)

    own, partner = len(ORDER) - 2, len(ORDER) - 1
    arrive(PAIRS - 1, 2)
    z_copy(partner, targets[partner]).start()
    mixed_in[own] = part[own, n_tp - 1]

    def taken(g):
        block = mixed_in[g * per_group : (g + 1) * per_group].reshape(per_group * cap, width)
        return jnp.dot(pick_hi[g], block, preferred_element_type=jnp.float32) + jnp.dot(
            pick_lo[g], block, preferred_element_type=jnp.float32
        )

    total = residual[...].astype(jnp.float32)
    for g in range(groups):
        for k in range(g * per_group, (g + 1) * per_group):
            if k != own:
                z_copy(k, targets[k]).wait_recv()
        total = total + taken(g)
    out[...] = total.astype(jnp.bfloat16)

    def drain(k, carry):
        for hop in range(3):
            pltpu.make_async_remote_copy(
                src_ref=part.at[k, 0], dst_ref=ring_in.at[hop, k],
                send_sem=ring_send.at[hop, k], recv_sem=ring_recv.at[hop, k],
                device_id={"tp": up}, device_id_type=MESH,
            ).wait_send()
        return carry

    lax.fori_loop(0, len(ORDER), drain, 0)
    for k in range(len(ORDER)):
        if k != own:
            z_copy(k, targets[k]).wait_send()


def on_device(hidden, down_weight, routes, route_weight, residual):
    sources, cap, units = hidden.shape[1:]
    tokens, width = residual.shape
    n_tp = len(SLICE_SHIFT)
    bf16 = jnp.bfloat16
    any_space = pl.BlockSpec(memory_space=pl.ANY)
    vmem = pl.BlockSpec(memory_space=pltpu.VMEM)
    groups = 4
    return pl.pallas_call(
        kernel,
        out_shape=jax.ShapeDtypeStruct((tokens, width), bf16),
        in_specs=[any_space, any_space, vmem, vmem, vmem],
        out_specs=vmem,
        scratch_shapes=[
            pltpu.VMEM((n_tp, units, width), bf16),
            pltpu.VMEM((sources, cap, units), bf16),
            pltpu.VMEM((sources, n_tp, cap, width), bf16),
            pltpu.VMEM((n_tp - 1, sources, cap, width), bf16),
            pltpu.VMEM((sources, cap, width), bf16),
            pltpu.VMEM((groups, tokens, sources // groups * cap), bf16),
            pltpu.VMEM((groups, tokens, sources // groups * cap), bf16),
            pltpu.SemaphoreType.DMA((n_tp,)),
            pltpu.SemaphoreType.DMA((sources,)),
            pltpu.SemaphoreType.DMA((n_tp - 1, sources)),
            pltpu.SemaphoreType.DMA((n_tp - 1, sources)),
            pltpu.SemaphoreType.DMA((sources,)),
            pltpu.SemaphoreType.DMA((sources,)),
        ],
        compiler_params=pltpu.CompilerParams(
            collective_id=0, has_side_effects=True, vmem_limit_bytes=60 * 1024 * 1024
        ),
        name="moe_down_combine",
    )(hidden, down_weight, routes, route_weight, residual)


def solution(mesh):
    return jax.shard_map(
        on_device,
        mesh=mesh,
        in_specs=(
            P("expert", "dp", None, "tp"),
            P("expert", "tp", None),
            P(("dp", "expert"), None),
            P(("dp", "expert"), None),
            P(("dp", "expert"), "tp"),
        ),
        out_specs=P(("dp", "expert"), "tp"),
        check_vma=False,
    )
```

time: 320 us -> 102 us (0.32)
  waiting for transfers between devices: 231 us -> 0 us
  Pallas kernels: 0 us -> 96.7 us
  local copies, waits for them, and re-layouts: 30 us -> 4.72 us
  matrix products: 20 us -> 0 us
  other arithmetic: 14.9 us -> 0 us
  between operations: 13.5 us -> 0.01 us
  starting transfers between devices: 10.2 us -> 0 us
    all_to_all x1 -> x0, waiting for transfers between devices: 204 us -> none  [on_device(): lax.all_to_all(partial_value, 'expert', split_axis=0, concat_axis=1, tile...]
    pallas_call x0 -> x1, Pallas kernels: none -> 96.7 us  [on_device(): pl.pallas_call(kernel, out_shape=jax.ShapeDtypeStruct((tokens, width), bf...]
    reduce_scatter x1 -> x0, waiting for transfers between devices: 27 us -> none  [on_device(): lax.psum_scatter(mixed_part.astype(jnp.bfloat16), 'tp', scatter_dimension...]
    dot_general x1 -> x0, matrix products: 20 us -> none  [on_device(): jnp.einsum('lsch,lhd->slcd', hidden, down_weight, preferred_element_type=...]
    gather x1 -> x0, local copies, waits for them, and re-layouts: 17.1 us -> none  [combine(): flattened[slot_index].astype(jnp.float32)]
    reduce_sum x4 -> x0, other arithmetic: 12.3 us -> none  [the longest x1 12.2 us: combine(): return jnp.sum(share[:, :, None] * picked, axis=1)]
    convert_element_type x1 -> x0, local copies, waits for them, and re-layouts: 12.2 us -> none  [combine(): flattened[slot_index].astype(jnp.float32)]
    all_to_all x1 -> x0, starting transfers between devices: 10.1 us -> none  [on_device(): lax.all_to_all(partial_value, 'expert', split_axis=0, concat_axis=1, tile...]
  transfers between devices with their start and end apart: 2 -> 0, of which waited for: 2 -> 0; matrix products, arithmetic and copies ran while one was open for 0% -> 0% of each run, Pallas kernels for 0% -> 0%
where the time goes in v1:
time: 102 us; the launch traced here: 101 us
  Pallas kernels  96.7 us (95%)
  local copies, waits for them, and re-layouts  4.72 us (5%)
    pallas_call x1, Pallas kernels, on_device(): pl.pallas_call(kernel, out_shape=jax.ShapeDtypeStruct((tokens, width), bf...  96.7 us
    unnamed x3, local copies, waits for them, and re-layouts  4.72 us

profile of v1, /device:TPU:1, one launch (start us, length us, event | category | flops | bytes accessed | tf_op | source)
XLA Modules:
  0.0 101.5 jit_solution(14928382294371990830)
XLA Ops:
  0.0 1.5 %copy.6.routes = s32[256,4]{1,0:T(8,128)} copy(s32[256,4]{0,1:T(4,128)} %param.7) | data formatting | bytes 8192 | tf_op args[2]
  1.5 1.5 %copy.7.route_weight = f32[256,4]{1,0:T(8,128)} copy(f32[256,4]{0,1:T(4,128)} %param.8) | data formatting | bytes 8192 | tf_op args[3]
  3.0 96.7 %moe_down_combine.1 = bf16[256,768]{1,0:T(8,128)(2,1)} custom-call(bf16[1,16,96,1408]{3,2,1,0:T(8,128)(2,1)} %hidden.1, bf16[1,1408,3072]{2,1,0:T(8,128)(2,1)} %weight.1, s32[256,4]{1,0:T(8,128)} %copy.6.routes, f32[256,4]{1,0:T(8,128)} %copy.7.route_weight, bf16[256,768]{1,0:T(8,128)(2,1)} %residual.1), custom_call_target="tpu_custom_call" | custom-call | tf_op jit(solution)/shard_map/moe_down_combine/pallas_call | solution.py:223
  99.7 1.8 %copy.9 = bf16[256,768]{1,0:T(8,128)(2,1)} copy(bf16[256,768]{1,0:T(8,128)(2,1)} %moe_down_combine.1) | data formatting | bytes 786432

commit v2 on v0

v2 whole, which is shorter than its diff:
```python
import jax
import jax.numpy as jnp
from jax import lax
from jax.experimental import pallas as pl
from jax.experimental.pallas import tpu as pltpu
from jax.sharding import PartitionSpec as P

MESH = pl.DeviceIdType.MESH

CHIPS = 8
LAST = CHIPS - 1
SLICE_SHIFT = (3, 1, 2, 0)
HOPS = ((0, 2, 1, 3), (1, 2, 0, 3))
TP_FIRST = 512
STREAM = 256


def kernel(
    hidden, weight, routes, scores, residual, out,
    w_buf, h_buf, part, ring_in, blocks, hand_b, hand_a, tok, tok_in, late, late_in,
    all_routes, all_scores, counts, table, pick_hi, pick_lo,
    w_sem, h_sem, ring_send, ring_recv, hb_send, hb_recv, ha_send, ha_recv, tok_send, tok_recv,
    late_send, late_recv, route_send, route_recv, score_send, score_recv,
):
    expert, tp = lax.axis_index("expert"), lax.axis_index("tp")
    n_tp = len(SLICE_SHIFT)
    cap, width = part.shape[2], residual.shape[1]
    tokens = residual.shape[0]
    half = tokens // 2
    f32, bf16 = jnp.float32, jnp.bfloat16
    z, core = expert // 2, lax.rem(expert, 2)
    up, down = lax.rem(tp + 1, n_tp), lax.rem(tp + n_tp - 1, n_tp)
    partner = 2 * z + 1 - core

    def chip(shift):
        return lax.rem(z + shift + CHIPS, CHIPS)

    def ahead(i):
        return (CHIPS // 2 - (i + 1) // 2) * (1 if i % 2 == 1 else -1)

    barrier = pltpu.get_barrier_semaphore()
    for peer in (up, down):
        pl.semaphore_signal(barrier, inc=1, device_id={"tp": peer}, device_id_type=MESH)
    pl.semaphore_signal(barrier, inc=1, device_id={"expert": partner}, device_id_type=MESH)
    for i in range(LAST):
        peer = 2 * chip(-ahead(i)) + core
        pl.semaphore_signal(barrier, inc=1, device_id={"expert": peer}, device_id_type=MESH)

    def w_load(r):
        start = pl.multiple_of(lax.rem(tp + SLICE_SHIFT[r], n_tp) * width, width)
        return pltpu.make_async_copy(weight.at[0, :, pl.ds(start, width)], w_buf.at[r], w_sem.at[r])

    def h_load(i, other):
        source = 2 * chip(ahead(i)) + (1 - core if other else core)
        return pltpu.make_async_copy(hidden.at[0, source], h_buf.at[2 * i + other], h_sem.at[2 * i + other])

    for other in range(2):
        h_load(0, other).start()
    for r in range(n_tp):
        w_load(r).start()
    for i in range(1, CHIPS):
        for other in range(2):
            h_load(i, other).start()

    def route_copies(i):
        peer = {"expert": 2 * chip(-ahead(i)) + core}
        return [
            pltpu.make_async_remote_copy(
                src_ref=src, dst_ref=dst.at[i], send_sem=send.at[i], recv_sem=recv.at[i],
                device_id=peer, device_id_type=MESH,
            )
            for src, dst, send, recv in (
                (routes, all_routes, route_send, route_recv),
                (scores, all_scores, score_send, score_recv),
            )
        ]

    def ring_copy(i, way, hop):
        k = 2 * i + way
        return pltpu.make_async_remote_copy(
            src_ref=part.at[k, HOPS[way][hop]],
            dst_ref=ring_in.at[hop, k],
            send_sem=ring_send.at[hop, k],
            recv_sem=ring_recv.at[hop, k],
            device_id={"tp": (up, down)[way]},
            device_id_type=MESH,
        )

    def late_copy(way, hop):
        return pltpu.make_async_remote_copy(
            src_ref=late.at[HOPS[way][hop], pl.ds(way * half, half)],
            dst_ref=late_in.at[hop, way],
            send_sem=late_send.at[hop, way],
            recv_sem=late_recv.at[hop, way],
            device_id={"tp": (up, down)[way]},
            device_id_type=MESH,
        )

    def hand_copy(i, early):
        first, count = (n_tp, TP_FIRST // STREAM) if early else (0, n_tp)
        source, send, recv = (hand_a, ha_send, ha_recv) if early else (hand_b, hb_send, hb_recv)
        return pltpu.make_async_remote_copy(
            src_ref=source.at[i],
            dst_ref=blocks.at[i, pl.ds(first, count), 1],
            send_sem=send.at[i],
            recv_sem=recv.at[i],
            device_id={"expert": partner},
            device_id_type=MESH,
        )

    def tok_copy(i, s, target):
        return pltpu.make_async_remote_copy(
            src_ref=tok.at[i, s],
            dst_ref=tok_in.at[i, s],
            send_sem=tok_send.at[i, s],
            recv_sem=tok_recv.at[i, s],
            device_id={"expert": 2 * target + core},
            device_id_type=MESH,
        )

    def left_rows(i):
        return h_buf[pl.ds(2 * i, 2)].reshape(2 * cap, h_buf.shape[2])

    def await_rows(i):
        for other in range(2):
            k = 2 * i + other
            pltpu.make_async_copy(hidden.at[0, 0], h_buf.at[k], h_sem.at[k]).wait()

    def matmul_early(i, first):
        left = left_rows(i)
        for r in range(n_tp):
            if first:
                w_load(r).wait()

            def tile(t, carry):
                at = pl.ds(pl.multiple_of(t * STREAM, STREAM), STREAM)
                product = jnp.dot(left, w_buf[r, :, at], preferred_element_type=f32)
                part[pl.ds(2 * i, 2), r, :, at] = product.astype(bf16).reshape(2, cap, STREAM)
                return carry

            lax.fori_loop(0, TP_FIRST // STREAM, tile, 0)
            if r == 1:
                if first:
                    pl.semaphore_wait(barrier, LAST + 3)
                ring_copy(i, 0, 0).start()
            if r == 2:
                ring_copy(i, 1, 0).start()

    def matmul_late(i, carry):
        left = left_rows(i)

        def tile(r, inner):
            product = jnp.dot(left, w_buf[r, :, TP_FIRST:], preferred_element_type=f32).astype(bf16)
            blocks[i, r, 0] = product[:cap]
            hand_b[i, r] = product[cap:]
            return inner

        lax.fori_loop(0, n_tp, tile, 0)
        hand_copy(i, False).start()
        return carry

    def arrive(i, hop):
        for way in range(2):
            ring_copy(i, way, hop).wait_recv()
        for way in range(2):
            k, r = 2 * i + way, HOPS[way][hop + 1]
            value = part[k, r] + ring_in[hop, k]
            if hop < n_tp - 2:
                part[k, r] = value
            else:
                for h in range(TP_FIRST // STREAM):
                    piece = value[:, h * STREAM : (h + 1) * STREAM]
                    if way == 0:
                        blocks[i, n_tp + h, 0] = piece
                    else:
                        hand_a[i, h] = piece

    def weighted(i, s):
        rows = blocks[i, s].reshape(2 * cap, STREAM)
        return jnp.dot(pick_hi[i], rows, preferred_element_type=f32) + jnp.dot(
            pick_lo[i], rows, preferred_element_type=f32
        )

    def chain(i, first, count, early):
        hand_copy(i, early).wait_recv()

        def one(s, carry):
            forward = (s < 2) | (s == n_tp)
            total = weighted(i, s)
            begins = (i == 0) | (i == jnp.where(forward, 2, 1))

            @pl.when(begins)
            def _():
                tok[i, s] = total.astype(bf16)

            @pl.when(jnp.logical_not(begins))
            def _():
                source = jnp.maximum(i - 2, 0)
                tok_copy(source, s, z).wait_recv()
                tok[i, s] = (total + tok_in[source, s].astype(f32)).astype(bf16)

            onward = jnp.where(i == 0, forward, lax.rem(i, 2) == 1)
            tok_copy(i, s, chip(jnp.where(onward, 1, -1))).start()
            return carry

        lax.fori_loop(first, first + count, one, 0)

    def chain_end(s):
        for i in (LAST - 2, LAST - 1):
            tok_copy(i, s, z).wait_recv()
        return weighted(LAST, s) + tok_in[LAST - 2, s].astype(f32) + tok_in[LAST - 1, s].astype(f32)

    def chain_late(i, carry):
        chain(i, 0, n_tp, False)
        return carry

    def chain_early(i, carry):
        chain(i, n_tp, TP_FIRST // STREAM, True)
        return carry

    await_rows(0)
    matmul_early(0, True)
    for i in range(LAST):
        for copy in route_copies(i):
            copy.start()
    all_routes[LAST] = routes[...]
    all_scores[LAST] = scores[...]
    matmul_late(0, 0)
    await_rows(1)
    matmul_early(1, False)
    await_rows(2)

    rows = lax.broadcasted_iota(jnp.int32, (tokens, tokens), 0)
    cols = lax.broadcasted_iota(jnp.int32, (tokens, tokens), 1)
    earlier = jnp.where(rows < cols, 1.0, 0.0).astype(bf16)
    for i in range(CHIPS):
        if i < LAST:
            for copy in route_copies(i):
                copy.wait_recv()
        chosen, value = all_routes[i], all_scores[i]
        share = value / jnp.sum(value, axis=0, keepdims=True)
        for q, e in enumerate((expert, partner)):
            same = chosen == e
            line = pl.ds(2 * i + q, 1)
            counts[line, :] = jnp.sum(jnp.where(same, 1.0, 0.0), axis=0, keepdims=True)
            table[pl.ds(4 * CHIPS + 2 * i + q, 1), :] = jnp.sum(jnp.where(same, share, 0.0), axis=0, keepdims=True)
    member = counts[...]
    before = jnp.dot(member.astype(bf16), earlier, preferred_element_type=f32)
    second = lax.rem(lax.broadcasted_iota(jnp.int32, member.shape, 0), 2) == 1
    portion = table[4 * CHIPS : 6 * CHIPS, :]
    portion_hi = portion.astype(bf16).astype(f32)
    table[0 : 2 * CHIPS, :] = jnp.where(member > 0.5, before + jnp.where(second, float(cap), 0.0), -1.0)
    table[2 * CHIPS : 4 * CHIPS, :] = portion_hi
    table[4 * CHIPS : 6 * CHIPS, :] = portion - portion_hi
    table[6 * CHIPS :, :] = jnp.zeros((table.shape[0] - 6 * CHIPS, tokens), f32)
    upright = jnp.transpose(table[...])
    column = lax.broadcasted_iota(jnp.int32, (tokens, 2 * cap), 1).astype(f32)
    for i in range(CHIPS):
        own, other = (
            column == upright[:, 2 * i + q : 2 * i + q + 1] for q in range(2)
        )
        for pick, base in ((pick_hi, 2 * CHIPS), (pick_lo, 4 * CHIPS)):
            a, b = (upright[:, base + 2 * i + q : base + 2 * i + q + 1] for q in range(2))
            pick[i] = jnp.where(own, a, jnp.where(other, b, 0.0)).astype(bf16)

    chain_late(0, 0)

    def step(n, carry):
        @pl.when(n + 2 < CHIPS)
        def _():
            await_rows(n + 2)

        @pl.when(n + 1 < CHIPS)
        def _():
            matmul_early(n + 1, False)

        for hop in range(n_tp - 1):
            i = n - 1 - hop

            @pl.when((i >= 0) & (i < CHIPS))
            def _():
                arrive(i, hop)
                if hop < n_tp - 2:
                    for way in range(2):
                        ring_copy(i, way, hop + 1).start()
                else:
                    hand_copy(i, True).start()

        odd = lax.rem(n, 2) == 1
        begin = jnp.where(n == 1, 1, jnp.where(odd, CHIPS, n + 1))
        end = jnp.where(n == 1, 3, jnp.minimum(n + 3, CHIPS))
        lax.fori_loop(begin, end, matmul_late, 0)
        lax.fori_loop(jnp.where(odd, n, LAST), jnp.minimum(n + 2, LAST), chain_late, 0)
        lax.fori_loop(jnp.where(odd, jnp.maximum(n - 4, 0), LAST), jnp.minimum(n - 2, LAST), chain_early, 0)

        @pl.when(n == LAST)
        def _():
            hand_copy(LAST, False).wait_recv()
            for s in range(n_tp):
                late[s] = chain_end(s).astype(bf16)
            for way in range(2):
                late_copy(way, 0).start()

        for hop in range(n_tp - 2):
            @pl.when(n == CHIPS + hop)
            def _():
                for way in range(2):
                    late_copy(way, hop).wait_recv()
                for way in range(2):
                    here = pl.ds(way * half, half)
                    r = HOPS[way][hop + 1]
                    late[r, here] = late[r, here] + late_in[hop, way]
                for way in range(2):
                    late_copy(way, hop + 1).start()

        return carry

    lax.fori_loop(1, CHIPS + n_tp - 1, step, 0)

    for way in range(2):
        late_copy(way, n_tp - 2).wait_recv()
        here = slice(way * half, (way + 1) * half)
        mixed = late[n_tp - 1, here].astype(f32) + late_in[n_tp - 2, way].astype(f32)
        out[here, TP_FIRST:] = (residual[here, TP_FIRST:].astype(f32) + mixed).astype(bf16)
    hand_copy(LAST, True).wait_recv()
    for h in range(TP_FIRST // STREAM):
        at = slice(h * STREAM, (h + 1) * STREAM)
        out[:, at] = (residual[:, at].astype(f32) + chain_end(n_tp + h)).astype(bf16)

    def drain(i, carry):
        for hop in range(n_tp - 1):
            for way in range(2):
                ring_copy(i, way, hop).wait_send()
        for early in (False, True):
            hand_copy(i, early).wait_send()

        @pl.when(i < LAST)
        def _():
            for s in range(blocks.shape[1]):
                tok_copy(i, s, z).wait_send()

        return carry

    lax.fori_loop(0, CHIPS, drain, 0)
    for i in range(LAST):
        for copy in route_copies(i):
            copy.wait_send()
    for hop in range(n_tp - 1):
        for way in range(2):
            late_copy(way, hop).wait_send()


def on_device(hidden, down_weight, routes, route_weight, residual):
    sources, cap, units = hidden.shape[1:]
    tokens, width = residual.shape
    top = routes.shape[1]
    n_tp = len(SLICE_SHIFT)
    early = TP_FIRST // STREAM
    streams = n_tp + early
    bf16, f32 = jnp.bfloat16, jnp.float32
    any_space = pl.BlockSpec(memory_space=pl.ANY)
    vmem = pl.BlockSpec(memory_space=pltpu.VMEM)
    dma = pltpu.SemaphoreType.DMA
    return pl.pallas_call(
        kernel,
        out_shape=jax.ShapeDtypeStruct((tokens, width), bf16),
        in_specs=[any_space, any_space, vmem, vmem, vmem],
        out_specs=vmem,
        scratch_shapes=[
            pltpu.VMEM((n_tp, units, width), bf16),
            pltpu.VMEM((sources, cap, units), bf16),
            pltpu.VMEM((sources, n_tp, cap, TP_FIRST), bf16),
            pltpu.VMEM((n_tp - 1, sources, cap, TP_FIRST), bf16),
            pltpu.VMEM((CHIPS, streams, 2, cap, STREAM), bf16),
            pltpu.VMEM((CHIPS, n_tp, cap, STREAM), bf16),
            pltpu.VMEM((CHIPS, early, cap, STREAM), bf16),
            pltpu.VMEM((LAST, streams, tokens, STREAM), bf16),
            pltpu.VMEM((LAST, streams, tokens, STREAM), bf16),
            pltpu.VMEM((n_tp, tokens, STREAM), bf16),
            pltpu.VMEM((n_tp - 1, 2, tokens // 2, STREAM), bf16),
            pltpu.VMEM((CHIPS, top, tokens), jnp.int32),
            pltpu.VMEM((CHIPS, top, tokens), f32),
            pltpu.VMEM((2 * CHIPS, tokens), f32),
            pltpu.VMEM((128, tokens), f32),
            pltpu.VMEM((CHIPS, tokens, 2 * cap), bf16),
            pltpu.VMEM((CHIPS, tokens, 2 * cap), bf16),
            dma((n_tp,)),
            dma((sources,)),
            dma((n_tp - 1, sources)),
            dma((n_tp - 1, sources)),
            dma((CHIPS,)),
            dma((CHIPS,)),
            dma((CHIPS,)),
            dma((CHIPS,)),
            dma((LAST, streams)),
            dma((LAST, streams)),
            dma((n_tp - 1, 2)),
            dma((n_tp - 1, 2)),
            dma((LAST,)),
            dma((LAST,)),
            dma((LAST,)),
            dma((LAST,)),
        ],
        compiler_params=pltpu.CompilerParams(
            collective_id=0, has_side_effects=True, vmem_limit_bytes=60 * 1024 * 1024
        ),
        name="moe_down_combine",
    )(hidden, down_weight, routes.T, route_weight.T, residual)


def solution(mesh):
    return jax.shard_map(
        on_device,
        mesh=mesh,
        in_specs=(
            P("expert", "dp", None, "tp"),
            P("expert", "tp", None),
            P(("dp", "expert"), None),
            P(("dp", "expert"), None),
            P(("dp", "expert"), "tp"),
        ),
        out_specs=P(("dp", "expert"), "tp"),
        check_vma=False,
    )
```

time: 320 us -> 96.5 us (0.30)
  waiting for transfers between devices: 231 us -> 0 us
  Pallas kernels: 0 us -> 94.6 us
  local copies, waits for them, and re-layouts: 30 us -> 1.77 us
  matrix products: 20 us -> 0 us
  other arithmetic: 14.9 us -> 0 us
  between operations: 13.5 us -> 0.01 us
  starting transfers between devices: 10.2 us -> 0 us
    all_to_all x1 -> x0, waiting for transfers between devices: 204 us -> none  [on_device(): lax.all_to_all(partial_value, 'expert', split_axis=0, concat_axis=1, tile...]
    pallas_call x0 -> x1, Pallas kernels: none -> 94.6 us  [on_device(): pl.pallas_call(kernel, out_shape=jax.ShapeDtypeStruct((tokens, width), bf...]
    reduce_scatter x1 -> x0, waiting for transfers between devices: 27 us -> none  [on_device(): lax.psum_scatter(mixed_part.astype(jnp.bfloat16), 'tp', scatter_dimension...]
    dot_general x1 -> x0, matrix products: 20 us -> none  [on_device(): jnp.einsum('lsch,lhd->slcd', hidden, down_weight, preferred_element_type=...]
    gather x1 -> x0, local copies, waits for them, and re-layouts: 17.1 us -> none  [combine(): flattened[slot_index].astype(jnp.float32)]
    reduce_sum x4 -> x0, other arithmetic: 12.3 us -> none  [the longest x1 12.2 us: combine(): return jnp.sum(share[:, :, None] * picked, axis=1)]
    convert_element_type x1 -> x0, local copies, waits for them, and re-layouts: 12.2 us -> none  [combine(): flattened[slot_index].astype(jnp.float32)]
    all_to_all x1 -> x0, starting transfers between devices: 10.1 us -> none  [on_device(): lax.all_to_all(partial_value, 'expert', split_axis=0, concat_axis=1, tile...]
  transfers between devices with their start and end apart: 2 -> 0, of which waited for: 2 -> 0; matrix products, arithmetic and copies ran while one was open for 0% -> 0% of each run, Pallas kernels for 0% -> 0%
where the time goes in v2:
time: 96.5 us; the launch traced here: 96.4 us
  Pallas kernels  94.6 us (98%)
  local copies, waits for them, and re-layouts  1.77 us (2%)
    pallas_call x1, Pallas kernels, on_device(): pl.pallas_call(kernel, out_shape=jax.ShapeDtypeStruct((tokens, width), bf...  94.6 us

profile of v2, /device:TPU:1, one launch (start us, length us, event | category | flops | bytes accessed | tf_op | source)
XLA Modules:
  0.0 96.4 jit_solution(1165217490801465301)
XLA Ops:
  0.0 94.6 %moe_down_combine.1 = bf16[256,768]{1,0:T(8,128)(2,1)} custom-call(bf16[1,16,96,1408]{3,2,1,0:T(8,128)(2,1)} %hidden.1, bf16[1,1408,3072]{2,1,0:T(8,128)(2,1)} %weight.1, s32[4,256]{1,0:T(4,128)} %bitcast.2, f32[4,256]{1,0:T(4,128)} %bitcast.3, bf16[256,768]{1,0:T(8,128)(2,1)} %residual.1), custom_call_target="tpu_custom_call" | custom-call | tf_op jit(solution)/shard_map/moe_down_combine/pallas_call | solution.py:364
  94.6 1.8 %copy.7 = bf16[256,768]{1,0:T(8,128)(2,1)} copy(bf16[256,768]{1,0:T(8,128)(2,1)} %moe_down_combine.1) | data formatting | bytes 786432

commit v3 on v2

v3 whole, which is shorter than its diff:
```python
import jax
import jax.numpy as jnp
from jax import lax
from jax.experimental import pallas as pl
from jax.experimental.pallas import tpu as pltpu
from jax.sharding import PartitionSpec as P

MESH = pl.DeviceIdType.MESH

CHIPS = 8
LAST = CHIPS - 1
SLICE_SHIFT = (3, 1, 2, 0)
HOPS = ((0, 2, 1, 3), (1, 2, 0, 3))
TP_FIRST = 512
STREAM = 256

ORDER = (
    64, 1, 2, 3, 8, 72, 9, 10, 11, 16, 80, 128, 384, 520, 528, 201, 209, 202,
    210, 203, 136, 211, 17, 18, 19, 24, 88, 25, 26, 27, 32, 96, 536, 33, 34, 144,
    217, 35, 544, 225, 137, 129, 40, 104, 152, 218, 226, 41, 42, 160, 43, 48, 112, 219,
    227, 145, 49, 50, 51, 56, 120, 552, 560, 57, 58, 59, 458, 450, 233, 241, 525, 153,
    234, 242, 168, 161, 235, 243, 466, 264, 532, 176, 204, 213, 184, 257, 474, 169, 541, 482,
    258, 177, 259, 320, 548, 185, 490, 220, 229, 498, 557, 321, 564, 506, 236, 245, 322,
)


WORDS = tuple(
    sum(code << 10 * j for j, code in enumerate(ORDER[t : t + 3])) for t in range(0, len(ORDER), 3)
)


def kernel(
    hidden, weight, routes, scores, residual, out,
    w_early, w_late, h_buf, part, ring_in, blocks, hand_b, hand_a, raw_in, tok, tok_in, late, late_in,
    all_routes, all_scores, counts, table, pick_hi, pick_lo,
    we_sem, wl_sem, h_sem, ring_send, ring_recv, hb_send, hb_recv, ha_send, ha_recv, raw_send, raw_recv,
    tok_send, tok_recv, late_send, late_recv, route_send, route_recv, score_send, score_recv,
):
    expert, tp = lax.axis_index("expert"), lax.axis_index("tp")
    n_tp = len(SLICE_SHIFT)
    n_early = TP_FIRST // STREAM
    cap, width = part.shape[2], residual.shape[1]
    tokens = residual.shape[0]
    half = tokens // 2
    f32, bf16 = jnp.float32, jnp.bfloat16
    z, core = expert // 2, lax.rem(expert, 2)
    up, down = lax.rem(tp + 1, n_tp), lax.rem(tp + n_tp - 1, n_tp)
    partner = 2 * z + 1 - core

    def chip(shift):
        return lax.rem(z + shift + CHIPS, CHIPS)

    def ahead(i):
        return (CHIPS // 2 - (i + 1) // 2) * (1 if i % 2 == 1 else -1)

    barrier = pltpu.get_barrier_semaphore()
    for peer in (up, down):
        pl.semaphore_signal(barrier, inc=1, device_id={"tp": peer}, device_id_type=MESH)
    greeted = [2 * chip(-ahead(i)) + core for i in range(1, LAST)]
    greeted += [partner, 2 * chip(1) + 1 - core, 2 * chip(-1) + 1 - core]
    for peer in greeted:
        pl.semaphore_signal(barrier, inc=1, device_id={"expert": peer}, device_id_type=MESH)

    def w_load(r, early):
        start = lax.rem(tp + SLICE_SHIFT[r], n_tp) * width
        if early:
            at = pl.ds(pl.multiple_of(start, STREAM), TP_FIRST)
            return pltpu.make_async_copy(weight.at[0, :, at], w_early.at[r], we_sem.at[r])
        at = pl.ds(pl.multiple_of(start + TP_FIRST, STREAM), STREAM)
        return pltpu.make_async_copy(
            weight.at[0, :, at], w_late.at[:, pl.ds(r * STREAM, STREAM)], wl_sem.at[r]
        )

    def h_load(i, other):
        source = 2 * chip(ahead(i)) + (1 - core if other else core)
        return pltpu.make_async_copy(hidden.at[0, source], h_buf.at[2 * i + other], h_sem.at[2 * i + other])

    for other in range(2):
        h_load(0, other).start()
    w_load(0, True).start()
    for r in range(n_tp):
        w_load(r, False).start()
    for r in range(1, n_tp):
        w_load(r, True).start()
    for i in range(1, CHIPS):
        for other in range(2):
            h_load(i, other).start()

    def route_copies(i):
        peer = {"expert": 2 * chip(-ahead(i)) + core}
        return [
            pltpu.make_async_remote_copy(
                src_ref=src, dst_ref=dst.at[i], send_sem=send.at[i], recv_sem=recv.at[i],
                device_id=peer, device_id_type=MESH,
            )
            for src, dst, send, recv in (
                (routes, all_routes, route_send, route_recv),
                (scores, all_scores, score_send, score_recv),
            )
        ]

    def ring_part(way, hop):
        first, second = HOPS[way][0], HOPS[way][2]
        return jnp.where(hop == 0, first, jnp.where(hop == 2, second, 2))

    def ring_copy(i, way, hop):
        k = 2 * i + way
        return pltpu.make_async_remote_copy(
            src_ref=part.at[k, ring_part(way, hop)],
            dst_ref=ring_in.at[hop, k],
            send_sem=ring_send.at[hop, k],
            recv_sem=ring_recv.at[hop, k],
            device_id={"tp": (up, down)[way]},
            device_id_type=MESH,
        )

    def late_copy(way, hop):
        return pltpu.make_async_remote_copy(
            src_ref=late.at[ring_part(way, hop), pl.ds(way * half, half)],
            dst_ref=late_in.at[hop, way],
            send_sem=late_send.at[hop, way],
            recv_sem=late_recv.at[hop, way],
            device_id={"tp": (up, down)[way]},
            device_id_type=MESH,
        )

    def hand_copy(i, early):
        first, count = (n_tp, n_early) if early else (0, n_tp)
        source, send, recv = (hand_a, ha_send, ha_recv) if early else (hand_b, hb_send, hb_recv)
        return pltpu.make_async_remote_copy(
            src_ref=source.at[i],
            dst_ref=blocks.at[i, pl.ds(first, count), 1],
            send_sem=send.at[i],
            recv_sem=recv.at[i],
            device_id={"expert": partner},
            device_id_type=MESH,
        )

    def goes_up(s):
        return s in (0, 1, n_tp)

    def raw_copy(s, other):
        source = (hand_b.at[0, s] if s < n_tp else hand_a.at[0, s - n_tp]) if other else blocks.at[0, s, 0]
        return pltpu.make_async_remote_copy(
            src_ref=source,
            dst_ref=raw_in.at[s, other],
            send_sem=raw_send.at[s, other],
            recv_sem=raw_recv.at[s, other],
            device_id={"expert": 2 * chip(1 if goes_up(s) else -1) + (1 - core if other else core)},
            device_id_type=MESH,
        )

    def raw_wait(s):
        for other in range(2):
            pltpu.make_async_remote_copy(
                src_ref=raw_in.at[s, other], dst_ref=raw_in.at[s, other],
                send_sem=raw_send.at[s, other], recv_sem=raw_recv.at[s, other],
                device_id={"expert": partner}, device_id_type=MESH,
            ).wait_recv()

    def tok_copy(i, s, target):
        return pltpu.make_async_remote_copy(
            src_ref=tok.at[i - 1, s],
            dst_ref=tok_in.at[i - 1, s],
            send_sem=tok_send.at[i - 1, s],
            recv_sem=tok_recv.at[i - 1, s],
            device_id={"expert": 2 * target + core},
            device_id_type=MESH,
        )

    def left_rows(i):
        return h_buf[pl.ds(2 * i, 2)].reshape(2 * cap, h_buf.shape[2])

    def await_rows(i):
        for other in range(2):
            k = 2 * i + other
            pltpu.make_async_copy(hidden.at[0, 0], h_buf.at[k], h_sem.at[k]).wait()

    def product_early(i, r):
        product = jnp.dot(left_rows(i), w_early[r], preferred_element_type=f32)
        part[pl.ds(2 * i, 2), r] = product.astype(bf16).reshape(2, cap, TP_FIRST)

    def matmul_early(i, r):
        for way in range(n_tp - 1):
            @pl.when((i == 0) & (r == way + 1))
            def _():
                w_load(way + 1, True).wait()

        @pl.when(r == 0)
        def _():
            await_rows(i)

        product_early(i, r)
        for way in range(2):
            @pl.when(r == way)
            def _():
                ring_copy(i, way, 0).start()

    def matmul_late(i, x):
        @pl.when(i == 0)
        def _():
            for r in range(n_tp):
                w_load(r, False).wait()

        product = jnp.dot(left_rows(i), w_late[...], preferred_element_type=f32).astype(bf16)
        for r in range(n_tp):
            piece = product[:, r * STREAM : (r + 1) * STREAM]
            blocks[i, r, 0] = piece[:cap]
            hand_b[i, r] = piece[cap:]

        @pl.when(i == 0)
        def _():
            for s in range(n_tp):
                for other in range(2):
                    raw_copy(s, other).start()

        @pl.when(i > 0)
        def _():
            hand_copy(i, False).start()

    def arrive(i, hop):
        for way in range(2):
            ring_copy(i, way, hop).wait_recv()
        for way in range(2):
            k, r = 2 * i + way, ring_part(way, hop + 1)
            part[k, r] = part[k, r] + ring_in[hop, k]
        for way in range(2):
            ring_copy(i, way, hop + 1).start()

    def arrive_last(i, x):
        hop = n_tp - 2
        for way in range(2):
            ring_copy(i, way, hop).wait_recv()
        for way in range(2):
            k = 2 * i + way
            for h in range(n_early):
                at = slice(h * STREAM, (h + 1) * STREAM)
                piece = part[k, n_tp - 1, :, at] + ring_in[hop, k, :, at]
                if way == 0:
                    blocks[i, n_tp + h, 0] = piece
                else:
                    hand_a[i, h] = piece

        @pl.when(i == 0)
        def _():
            for s in range(n_tp, n_tp + n_early):
                for other in range(2):
                    raw_copy(s, other).start()

        @pl.when(i > 0)
        def _():
            hand_copy(i, True).start()

    def pick(j, rows):
        return jnp.dot(pick_hi[j], rows, preferred_element_type=f32) + jnp.dot(
            pick_lo[j], rows, preferred_element_type=f32
        )

    def weighted(i, s):
        return pick(i, blocks[i, s].reshape(2 * cap, STREAM))

    def chain(i, s):
        total = weighted(i, s)
        forward = (s < 2) | (s == n_tp)

        @pl.when(i > 2)
        def _():
            tok_copy(i - 2, s, z).wait_recv()
            tok[i - 1, s] = (total + tok_in[i - 3, s].astype(f32)).astype(bf16)

        raw = i == jnp.where(forward, 1, 2)

        @pl.when(raw)
        def _():
            raw_wait(s)
            more = pick(jnp.where(forward, 0, CHIPS), raw_in[s].reshape(2 * cap, STREAM))
            tok[i - 1, s] = (total + more).astype(bf16)

        @pl.when((i < 3) & jnp.logical_not(raw))
        def _():
            tok[i - 1, s] = total.astype(bf16)

        tok_copy(i, s, chip(jnp.where(lax.rem(i, 2) == 1, 1, -1))).start()

    def chain_first(i, s):
        @pl.when(s < n_tp)
        def _():
            hand_copy(i, False).wait_recv()

        @pl.when(s >= n_tp)
        def _():
            hand_copy(i, True).wait_recv()

        chain(i, s)

    def chain_end(s):
        for i in (LAST - 2, LAST - 1):
            tok_copy(i, s, z).wait_recv()
        return weighted(LAST, s) + tok_in[LAST - 3, s].astype(f32) + tok_in[LAST - 2, s].astype(f32)

    def end_late(first, s):
        @pl.when(first == 1)
        def _():
            hand_copy(LAST, False).wait_recv()

        late[s] = chain_end(s).astype(bf16)

    def late_step(i, x):
        @pl.when(x > 0)
        def _():
            for way in range(2):
                late_copy(way, x - 1).wait_recv()
            for way in range(2):
                here = pl.ds(way * half, half)
                r = ring_part(way, x)
                late[r, here] = late[r, here] + late_in[x - 1, way]

        for way in range(2):
            late_copy(way, x).start()

    def selection(i, x):
        rows = lax.broadcasted_iota(jnp.int32, (tokens, tokens), 0)
        cols = lax.broadcasted_iota(jnp.int32, (tokens, tokens), 1)
        earlier = jnp.where(rows < cols, 1.0, 0.0).astype(bf16)
        sets = CHIPS + 1
        for j in range(1, LAST):
            for copy in route_copies(j):
                copy.wait_recv()
        for j in range(sets):
            group, shift = ((1, -1) if j == 0 else (2, 1) if j == CHIPS else (j, 0))
            chosen, value = all_routes[group], all_scores[group]
            share = value / jnp.sum(value, axis=0, keepdims=True)
            for q in range(2):
                same = chosen == 2 * chip(shift) + (1 - core if q else core)
                line = 2 * j + q
                counts[line : line + 1, :] = jnp.sum(jnp.where(same, 1.0, 0.0), axis=0, keepdims=True)
                table[96 + line : 97 + line, :] = jnp.sum(jnp.where(same, share, 0.0), axis=0, keepdims=True)
        counts[2 * sets :, :] = jnp.zeros((counts.shape[0] - 2 * sets, tokens), f32)
        table[96 + 2 * sets :, :] = jnp.zeros((32 - 2 * sets, tokens), f32)
        member = counts[...]
        before = jnp.dot(member.astype(bf16), earlier, preferred_element_type=f32)
        second = lax.rem(lax.broadcasted_iota(jnp.int32, member.shape, 0), 2) == 1
        portion = table[96:128, :]
        portion_hi = portion.astype(bf16).astype(f32)
        table[0:32, :] = jnp.where(member > 0.5, before + jnp.where(second, float(cap), 0.0), -1.0)
        table[32:64, :] = portion_hi
        table[64:96, :] = portion - portion_hi
        upright = jnp.transpose(table[...])
        column = lax.broadcasted_iota(jnp.int32, (tokens, 2 * cap), 1).astype(f32)
        for j in range(sets):
            own, other = (column == upright[:, 2 * j + q : 2 * j + q + 1] for q in range(2))
            for target, base in ((pick_hi, 32), (pick_lo, 64)):
                a, b = (upright[:, base + 2 * j + q : base + 2 * j + q + 1] for q in range(2))
                target[j] = jnp.where(own, a, jnp.where(other, b, 0.0)).astype(bf16)

    kinds = (
        matmul_early, matmul_late, arrive, chain, end_late, late_step, selection, arrive_last, chain_first,
    )

    w_load(0, True).wait()
    await_rows(0)
    product_early(0, 0)
    pl.semaphore_wait(barrier, 2 + len(greeted))
    for i in range(1, LAST):
        for copy in route_copies(i):
            copy.start()
    ring_copy(0, 0, 0).start()
    all_routes[LAST] = routes[...]
    all_scores[LAST] = scores[...]

    def step(t, carry):
        word = jnp.int32(WORDS[0])
        for j in range(1, len(WORDS)):
            word = jnp.where(t >= 3 * j, WORDS[j], word)
        code = lax.rem(lax.shift_right_logical(word, 10 * lax.rem(t, 3)), 1024)
        i, x = lax.rem(code // 8, 8), lax.rem(code, 8)

        def branch(kind):
            def run():
                kind(i, x)

            return run

        lax.switch(code // 64, [branch(kind) for kind in kinds])
        return carry

    lax.fori_loop(0, len(ORDER), step, 0)

    for way in range(2):
        late_copy(way, n_tp - 2).wait_recv()
        here = slice(way * half, (way + 1) * half)
        mixed = late[n_tp - 1, here].astype(f32) + late_in[n_tp - 2, way].astype(f32)
        out[here, TP_FIRST:] = (residual[here, TP_FIRST:].astype(f32) + mixed).astype(bf16)
    hand_copy(LAST, True).wait_recv()
    for h in range(n_early):
        at = slice(h * STREAM, (h + 1) * STREAM)
        out[:, at] = (residual[:, at].astype(f32) + chain_end(n_tp + h)).astype(bf16)

    def drain(i, carry):
        for hop in range(n_tp - 1):
            for way in range(2):
                ring_copy(i, way, hop).wait_send()

        @pl.when(i > 0)
        def _():
            for early in (False, True):
                hand_copy(i, early).wait_send()

        @pl.when((i > 0) & (i < LAST))
        def _():
            for s in range(blocks.shape[1]):
                tok_copy(i, s, z).wait_send()

        return carry

    lax.fori_loop(0, CHIPS, drain, 0)
    for s in range(blocks.shape[1]):
        for other in range(2):
            raw_copy(s, other).wait_send()
    for i in range(1, LAST):
        for copy in route_copies(i):
            copy.wait_send()
    for hop in range(n_tp - 1):
        for way in range(2):
            late_copy(way, hop).wait_send()


def on_device(hidden, down_weight, routes, route_weight, residual):
    sources, cap, units = hidden.shape[1:]
    tokens, width = residual.shape
    top = routes.shape[1]
    n_tp = len(SLICE_SHIFT)
    early = TP_FIRST // STREAM
    streams = n_tp + early
    bf16, f32 = jnp.bfloat16, jnp.float32
    any_space = pl.BlockSpec(memory_space=pl.ANY)
    vmem = pl.BlockSpec(memory_space=pltpu.VMEM)
    dma = pltpu.SemaphoreType.DMA
    return pl.pallas_call(
        kernel,
        out_shape=jax.ShapeDtypeStruct((tokens, width), bf16),
        in_specs=[any_space, any_space, vmem, vmem, vmem],
        out_specs=vmem,
        scratch_shapes=[
            pltpu.VMEM((n_tp, units, TP_FIRST), bf16),
            pltpu.VMEM((units, n_tp * STREAM), bf16),
            pltpu.VMEM((sources, cap, units), bf16),
            pltpu.VMEM((sources, n_tp, cap, TP_FIRST), bf16),
            pltpu.VMEM((n_tp - 1, sources, cap, TP_FIRST), bf16),
            pltpu.VMEM((CHIPS, streams, 2, cap, STREAM), bf16),
            pltpu.VMEM((CHIPS, n_tp, cap, STREAM), bf16),
            pltpu.VMEM((CHIPS, early, cap, STREAM), bf16),
            pltpu.VMEM((streams, 2, cap, STREAM), bf16),
            pltpu.VMEM((LAST - 1, streams, tokens, STREAM), bf16),
            pltpu.VMEM((LAST - 1, streams, tokens, STREAM), bf16),
            pltpu.VMEM((n_tp, tokens, STREAM), bf16),
            pltpu.VMEM((n_tp - 1, 2, tokens // 2, STREAM), bf16),
            pltpu.VMEM((CHIPS, top, tokens), jnp.int32),
            pltpu.VMEM((CHIPS, top, tokens), f32),
            pltpu.VMEM((32, tokens), f32),
            pltpu.VMEM((128, tokens), f32),
            pltpu.VMEM((CHIPS + 1, tokens, 2 * cap), bf16),
            pltpu.VMEM((CHIPS + 1, tokens, 2 * cap), bf16),
            dma((n_tp,)),
            dma((n_tp,)),
            dma((sources,)),
            dma((n_tp - 1, sources)),
            dma((n_tp - 1, sources)),
            dma((CHIPS,)),
            dma((CHIPS,)),
            dma((CHIPS,)),
            dma((CHIPS,)),
            dma((streams, 2)),
            dma((streams, 2)),
            dma((LAST - 1, streams)),
            dma((LAST - 1, streams)),
            dma((n_tp - 1, 2)),
            dma((n_tp - 1, 2)),
            dma((LAST,)),
            dma((LAST,)),
            dma((LAST,)),
            dma((LAST,)),
        ],
        compiler_params=pltpu.CompilerParams(
            collective_id=0, has_side_effects=True, vmem_limit_bytes=60 * 1024 * 1024
        ),
        name="moe_down_combine",
    )(hidden, down_weight, routes.T, route_weight.T, residual)


def solution(mesh):
    return jax.shard_map(
        on_device,
        mesh=mesh,
        in_specs=(
            P("expert", "dp", None, "tp"),
            P("expert", "tp", None),
            P(("dp", "expert"), None),
            P(("dp", "expert"), None),
            P(("dp", "expert"), "tp"),
        ),
        out_specs=P(("dp", "expert"), "tp"),
        check_vma=False,
    )
```

time: 96.5 us -> 82.6 us (0.86)
  Pallas kernels: 94.6 us -> 80.7 us
    pallas_call x1, Pallas kernels: 94.6 us -> 80.7 us  [on_device(): pl.pallas_call(kernel, out_shape=jax.ShapeDtypeStruct((tokens, width), bf...]
where the time goes in v3:
time: 82.6 us; the launch traced here: 82.5 us
  Pallas kernels  80.7 us (98%)
  local copies, waits for them, and re-layouts  1.77 us (2%)
    pallas_call x1, Pallas kernels, on_device(): pl.pallas_call(kernel, out_shape=jax.ShapeDtypeStruct((tokens, width), bf...  80.7 us
    unnamed x1, local copies, waits for them, and re-layouts  1.77 us

profile of v3, /device:TPU:1, one launch (start us, length us, event | category | flops | bytes accessed | tf_op | source)
XLA Modules:
  0.0 82.5 jit_solution(3442022911748520745)
XLA Ops:
  0.0 80.7 %moe_down_combine.1 = bf16[256,768]{1,0:T(8,128)(2,1)} custom-call(bf16[1,16,96,1408]{3,2,1,0:T(8,128)(2,1)} %hidden.1, bf16[1,1408,3072]{2,1,0:T(8,128)(2,1)} %weight.1, s32[4,256]{1,0:T(4,128)} %bitcast.2, f32[4,256]{1,0:T(4,128)} %bitcast.3, bf16[256,768]{1,0:T(8,128)(2,1)} %residual.1), custom_call_target="tpu_custom_call" | custom-call | tf_op jit(solution)/shard_map/moe_down_combine/pallas_call | solution.py:439
  80.7 1.8 %copy.7 = bf16[256,768]{1,0:T(8,128)(2,1)} copy(bf16[256,768]{1,0:T(8,128)(2,1)} %moe_down_combine.1) | data formatting | bytes 786432

commit v4 on v3

--- a/solution.py
+++ b/solution.py
@@ -14,16 +14,16 @@
 TP_FIRST = 512
 STREAM = 256
 
+SETS = ((1, -1), (1, 0), (2, 0), (3, 0), (4, 0), (5, 0), (6, 0), (7, 0), (2, 1), (3, -1), (4, 1))
+
 ORDER = (
-    64, 1, 2, 3, 8, 72, 9, 10, 11, 16, 80, 128, 384, 520, 528, 201, 209, 202,
-    210, 203, 136, 211, 17, 18, 19, 24, 88, 25, 26, 27, 32, 96, 536, 33, 34, 144,
-    217, 35, 544, 225, 137, 129, 40, 104, 152, 218, 226, 41, 42, 160, 43, 48, 112, 219,
-    227, 145, 49, 50, 51, 56, 120, 552, 560, 57, 58, 59, 458, 450, 233, 241, 525, 153,
-    234, 242, 168, 161, 235, 243, 466, 264, 532, 176, 204, 213, 184, 257, 474, 169, 541, 482,
-    258, 177, 259, 320, 548, 185, 490, 220, 229, 498, 557, 321, 564, 506, 236, 245, 322,
+    1, 2, 3, 8, 9, 16, 17, 18, 19, 10, 11, 128, 72, 80, 136, 384, 385, 144,
+    521, 531, 210, 386, 200, 129, 24, 88, 32, 137, 96, 33, 538, 145, 219, 217, 544, 227,
+    225, 34, 387, 25, 40, 226, 104, 41, 42, 43, 160, 26, 554, 27, 458, 450, 216, 235,
+    35, 48, 49, 50, 152, 51, 233, 466, 112, 168, 56, 120, 57, 560, 243, 242, 161, 241,
+    58, 59, 176, 533, 524, 153, 169, 232, 184, 267, 482, 548, 177, 258, 474, 257, 540, 221,
+    490, 256, 320, 229, 185, 498, 556, 321, 564, 237, 245, 506, 322, 576, 576,
 )
-
-
 WORDS = tuple(
     sum(code << 10 * j for j, code in enumerate(ORDER[t : t + 3])) for t in range(0, len(ORDER), 3)
 )
@@ -32,7 +32,7 @@
 def kernel(
     hidden, weight, routes, scores, residual, out,
     w_early, w_late, h_buf, part, ring_in, blocks, hand_b, hand_a, raw_in, tok, tok_in, late, late_in,
-    all_routes, all_scores, counts, table, pick_hi, pick_lo,
+    all_routes, all_scores, counts, table, upright, pick_hi, pick_lo,
     we_sem, wl_sem, h_sem, ring_send, ring_recv, hb_send, hb_recv, ha_send, ha_recv, raw_send, raw_recv,
     tok_send, tok_recv, late_send, late_recv, route_send, route_recv, score_send, score_recv,
 ):
@@ -77,10 +77,9 @@
 
     for other in range(2):
         h_load(0, other).start()
-    w_load(0, True).start()
     for r in range(n_tp):
         w_load(r, False).start()
-    for r in range(1, n_tp):
+    for r in range(n_tp):
         w_load(r, True).start()
     for i in range(1, CHIPS):
         for other in range(2):
@@ -139,22 +138,34 @@
     def goes_up(s):
         return s in (0, 1, n_tp)
 
-    def raw_copy(s, other):
-        source = (hand_b.at[0, s] if s < n_tp else hand_a.at[0, s - n_tp]) if other else blocks.at[0, s, 0]
+    def raw_from(stage, s):
+        return 0 if stage == 0 else 2 if goes_up(s) else 1
+
+    def raw_copy(stage, s, other):
+        i = raw_from(stage, s)
+        source = (hand_b.at[i, s] if s < n_tp else hand_a.at[i, s - n_tp]) if other else blocks.at[i, s, 0]
+        target = chip(1 if goes_up(s) == (stage == 0) else -1)
         return pltpu.make_async_remote_copy(
             src_ref=source,
-            dst_ref=raw_in.at[s, other],
-            send_sem=raw_send.at[s, other],
-            recv_sem=raw_recv.at[s, other],
-            device_id={"expert": 2 * chip(1 if goes_up(s) else -1) + (1 - core if other else core)},
+            dst_ref=raw_in.at[stage, s, other],
+            send_sem=raw_send.at[stage, s, other],
+            recv_sem=raw_recv.at[stage, s, other],
+            device_id={"expert": 2 * target + (1 - core if other else core)},
             device_id_type=MESH,
         )
 
-    def raw_wait(s):
+    def raw_start(i, streams):
+        for stage in range(2):
+            chosen = [s for s in streams if raw_from(stage, s) == i]
+            for s in chosen:
+                for other in range(2):
+                    raw_copy(stage, s, other).start()
+
+    def raw_wait(stage, s):
         for other in range(2):
             pltpu.make_async_remote_copy(
-                src_ref=raw_in.at[s, other], dst_ref=raw_in.at[s, other],
-                send_sem=raw_send.at[s, other], recv_sem=raw_recv.at[s, other],
+                src_ref=raw_in.at[stage, s, other], dst_ref=raw_in.at[stage, s, other],
+                send_sem=raw_send.at[stage, s, other], recv_sem=raw_recv.at[stage, s, other],
                 device_id={"expert": partner}, device_id_type=MESH,
             ).wait_recv()
 
@@ -196,27 +207,21 @@
             def _():
                 ring_copy(i, way, 0).start()
 
-    def matmul_late(i, x):
-        @pl.when(i == 0)
-        def _():
-            for r in range(n_tp):
-                w_load(r, False).wait()
-
+    def product_late(i):
         product = jnp.dot(left_rows(i), w_late[...], preferred_element_type=f32).astype(bf16)
         for r in range(n_tp):
             piece = product[:, r * STREAM : (r + 1) * STREAM]
             blocks[i, r, 0] = piece[:cap]
             hand_b[i, r] = piece[cap:]
 
-        @pl.when(i == 0)
-        def _():
-            for s in range(n_tp):
-                for other in range(2):
-                    raw_copy(s, other).start()
-
-        @pl.when(i > 0)
-        def _():
-            hand_copy(i, False).start()
+    def matmul_late(i, x):
+        product_late(i)
+        for begin in (1, 2):
+            @pl.when(i == begin)
+            def _():
+                raw_start(begin, range(n_tp))
+
+        hand_copy(i, False).start()
 
     def arrive(i, hop):
         for way in range(2):
@@ -241,11 +246,10 @@
                 else:
                     hand_a[i, h] = piece
 
-        @pl.when(i == 0)
-        def _():
-            for s in range(n_tp, n_tp + n_early):
-                for other in range(2):
-                    raw_copy(s, other).start()
+        for begin in range(3):
+            @pl.when(i == begin)
+            def _():
+                raw_start(begin, range(n_tp, n_tp + n_early))
 
         @pl.when(i > 0)
         def _():
@@ -262,24 +266,20 @@
     def chain(i, s):
         total = weighted(i, s)
         forward = (s < 2) | (s == n_tp)
-
-        @pl.when(i > 2)
+        raw = (i == jnp.where(forward, 1, 2)) | (i == jnp.where(forward, 4, 3))
+
+        @pl.when(raw)
+        def _():
+            stage = jnp.where(i > 2, 1, 0)
+            raw_wait(stage, s)
+            more = pick(jnp.where(i == 1, 0, i + LAST - 1), raw_in[stage, s].reshape(2 * cap, STREAM))
+            tok[i - 1, s] = (total + more).astype(bf16)
+
+        @pl.when(jnp.logical_not(raw))
         def _():
             tok_copy(i - 2, s, z).wait_recv()
             tok[i - 1, s] = (total + tok_in[i - 3, s].astype(f32)).astype(bf16)
 
-        raw = i == jnp.where(forward, 1, 2)
-
-        @pl.when(raw)
-        def _():
-            raw_wait(s)
-            more = pick(jnp.where(forward, 0, CHIPS), raw_in[s].reshape(2 * cap, STREAM))
-            tok[i - 1, s] = (total + more).astype(bf16)
-
-        @pl.when((i < 3) & jnp.logical_not(raw))
-        def _():
-            tok[i - 1, s] = total.astype(bf16)
-
         tok_copy(i, s, chip(jnp.where(lax.rem(i, 2) == 1, 1, -1))).start()
 
     def chain_first(i, s):
@@ -293,17 +293,17 @@
 
         chain(i, s)
 
-    def chain_end(s):
+    def chain_end(s, total):
         for i in (LAST - 2, LAST - 1):
             tok_copy(i, s, z).wait_recv()
-        return weighted(LAST, s) + tok_in[LAST - 3, s].astype(f32) + tok_in[LAST - 2, s].astype(f32)
+        return total + tok_in[LAST - 3, s].astype(f32) + tok_in[LAST - 2, s].astype(f32)
 
     def end_late(first, s):
         @pl.when(first == 1)
         def _():
             hand_copy(LAST, False).wait_recv()
 
-        late[s] = chain_end(s).astype(bf16)
+        late[s] = chain_end(s, weighted(LAST, s)).astype(bf16)
 
     def late_step(i, x):
         @pl.when(x > 0)
@@ -318,16 +318,14 @@
         for way in range(2):
             late_copy(way, x).start()
 
-    def selection(i, x):
+    def selection_table():
         rows = lax.broadcasted_iota(jnp.int32, (tokens, tokens), 0)
         cols = lax.broadcasted_iota(jnp.int32, (tokens, tokens), 1)
         earlier = jnp.where(rows < cols, 1.0, 0.0).astype(bf16)
-        sets = CHIPS + 1
         for j in range(1, LAST):
             for copy in route_copies(j):
                 copy.wait_recv()
-        for j in range(sets):
-            group, shift = ((1, -1) if j == 0 else (2, 1) if j == CHIPS else (j, 0))
+        for j, (group, shift) in enumerate(SETS):
             chosen, value = all_routes[group], all_scores[group]
             share = value / jnp.sum(value, axis=0, keepdims=True)
             for q in range(2):
@@ -335,8 +333,9 @@
                 line = 2 * j + q
                 counts[line : line + 1, :] = jnp.sum(jnp.where(same, 1.0, 0.0), axis=0, keepdims=True)
                 table[96 + line : 97 + line, :] = jnp.sum(jnp.where(same, share, 0.0), axis=0, keepdims=True)
-        counts[2 * sets :, :] = jnp.zeros((counts.shape[0] - 2 * sets, tokens), f32)
-        table[96 + 2 * sets :, :] = jnp.zeros((32 - 2 * sets, tokens), f32)
+        used = 2 * len(SETS)
+        counts[used:, :] = jnp.zeros((counts.shape[0] - used, tokens), f32)
+        table[96 + used :, :] = jnp.zeros((32 - used, tokens), f32)
         member = counts[...]
         before = jnp.dot(member.astype(bf16), earlier, preferred_element_type=f32)
         second = lax.rem(lax.broadcasted_iota(jnp.int32, member.shape, 0), 2) == 1
@@ -345,46 +344,68 @@
         table[0:32, :] = jnp.where(member > 0.5, before + jnp.where(second, float(cap), 0.0), -1.0)
         table[32:64, :] = portion_hi
         table[64:96, :] = portion - portion_hi
-        upright = jnp.transpose(table[...])
+        upright[...] = jnp.transpose(table[...])
+
+    def selection_sets(sets):
         column = lax.broadcasted_iota(jnp.int32, (tokens, 2 * cap), 1).astype(f32)
-        for j in range(sets):
+        for j in sets:
             own, other = (column == upright[:, 2 * j + q : 2 * j + q + 1] for q in range(2))
             for target, base in ((pick_hi, 32), (pick_lo, 64)):
                 a, b = (upright[:, base + 2 * j + q : base + 2 * j + q + 1] for q in range(2))
                 target[j] = jnp.where(own, a, jnp.where(other, b, 0.0)).astype(bf16)
 
+    def selection(i, x):
+        pl.when(x == 0)(selection_table)
+        for stage, sets in enumerate(((0, 8, 1, 2), (3, 4, 9, 10), (5, 6, 7))):
+            @pl.when(x == stage + 1)
+            def _():
+                selection_sets(sets)
+
+    def nothing(i, x):
+        pass
+
     kinds = (
         matmul_early, matmul_late, arrive, chain, end_late, late_step, selection, arrive_last, chain_first,
+        nothing,
     )
 
+    await_rows(0)
+    for r in range(n_tp):
+        w_load(r, False).wait()
+    product_late(0)
     w_load(0, True).wait()
-    await_rows(0)
     product_early(0, 0)
     pl.semaphore_wait(barrier, 2 + len(greeted))
     for i in range(1, LAST):
         for copy in route_copies(i):
             copy.start()
+    raw_start(0, range(n_tp))
     ring_copy(0, 0, 0).start()
     all_routes[LAST] = routes[...]
     all_scores[LAST] = scores[...]
 
-    def step(t, carry):
+    def steps(j, carry):
         word = jnp.int32(WORDS[0])
-        for j in range(1, len(WORDS)):
-            word = jnp.where(t >= 3 * j, WORDS[j], word)
-        code = lax.rem(lax.shift_right_logical(word, 10 * lax.rem(t, 3)), 1024)
-        i, x = lax.rem(code // 8, 8), lax.rem(code, 8)
-
-        def branch(kind):
-            def run():
-                kind(i, x)
-
-            return run
-
-        lax.switch(code // 64, [branch(kind) for kind in kinds])
+        for n in range(1, len(WORDS)):
+            word = jnp.where(j == n, WORDS[n], word)
+
+        def step(m, inner):
+            code = lax.rem(lax.shift_right_logical(word, 10 * m), 1024)
+            i, x = lax.rem(code // 8, 8), lax.rem(code, 8)
+
+            def branch(kind):
+                def run():
+                    kind(i, x)
+
+                return run
+
+            lax.switch(code // 64, [branch(kind) for kind in kinds])
+            return inner
+
+        lax.fori_loop(0, 3, step, 0)
         return carry
 
-    lax.fori_loop(0, len(ORDER), step, 0)
+    lax.fori_loop(0, len(WORDS), steps, 0)
 
     for way in range(2):
         late_copy(way, n_tp - 2).wait_recv()
@@ -392,9 +413,10 @@
         mixed = late[n_tp - 1, here].astype(f32) + late_in[n_tp - 2, way].astype(f32)
         out[here, TP_FIRST:] = (residual[here, TP_FIRST:].astype(f32) + mixed).astype(bf16)
     hand_copy(LAST, True).wait_recv()
+    totals = [weighted(LAST, n_tp + h) for h in range(n_early)]
     for h in range(n_early):
         at = slice(h * STREAM, (h + 1) * STREAM)
-        out[:, at] = (residual[:, at].astype(f32) + chain_end(n_tp + h)).astype(bf16)
+        out[:, at] = (residual[:, at].astype(f32) + chain_end(n_tp + h, totals[h])).astype(bf16)
 
     def drain(i, carry):
         for hop in range(n_tp - 1):
@@ -409,14 +431,17 @@
         @pl.when((i > 0) & (i < LAST))
         def _():
             for s in range(blocks.shape[1]):
-                tok_copy(i, s, z).wait_send()
+                @pl.when(i != (2 if goes_up(s) else 1))
+                def _():
+                    tok_copy(i, s, z).wait_send()
 
         return carry
 
     lax.fori_loop(0, CHIPS, drain, 0)
-    for s in range(blocks.shape[1]):
-        for other in range(2):
-            raw_copy(s, other).wait_send()
+    for stage in range(2):
+        for s in range(blocks.shape[1]):
+            for other in range(2):
+                raw_copy(stage, s, other).wait_send()
     for i in range(1, LAST):
         for copy in route_copies(i):
             copy.wait_send()
@@ -450,7 +475,7 @@
             pltpu.VMEM((CHIPS, streams, 2, cap, STREAM), bf16),
             pltpu.VMEM((CHIPS, n_tp, cap, STREAM), bf16),
             pltpu.VMEM((CHIPS, early, cap, STREAM), bf16),
-            pltpu.VMEM((streams, 2, cap, STREAM), bf16),
+            pltpu.VMEM((2, streams, 2, cap, STREAM), bf16),
             pltpu.VMEM((LAST - 1, streams, tokens, STREAM), bf16),
             pltpu.VMEM((LAST - 1, streams, tokens, STREAM), bf16),
             pltpu.VMEM((n_tp, tokens, STREAM), bf16),
@@ -459,8 +484,9 @@
             pltpu.VMEM((CHIPS, top, tokens), f32),
             pltpu.VMEM((32, tokens), f32),
             pltpu.VMEM((128, tokens), f32),
-            pltpu.VMEM((CHIPS + 1, tokens, 2 * cap), bf16),
-            pltpu.VMEM((CHIPS + 1, tokens, 2 * cap), bf16),
+            pltpu.VMEM((tokens, 128), f32),
+            pltpu.VMEM((len(SETS), tokens, 2 * cap), bf16),
+            pltpu.VMEM((len(SETS), tokens, 2 * cap), bf16),
             dma((n_tp,)),
             dma((n_tp,)),
             dma((sources,)),
@@ -470,8 +496,8 @@
             dma((CHIPS,)),
             dma((CHIPS,)),
             dma((CHIPS,)),
-            dma((streams, 2)),
-            dma((streams, 2)),
+            dma((2, streams, 2)),
+            dma((2, streams, 2)),
             dma((LAST - 1, streams)),
             dma((LAST - 1, streams)),
             dma((n_tp - 1, 2)),

time: 82.6 us -> 79.4 us (0.961)
  Pallas kernels: 80.7 us -> 77.2 us
    pallas_call x1, Pallas kernels: 80.7 us -> 77.2 us  [on_device(): pl.pallas_call(kernel, out_shape=jax.ShapeDtypeStruct((tokens, width), bf...]
where the time goes in v4:
time: 79.4 us; the launch traced here: 79 us
  Pallas kernels  77.2 us (97%)
  local copies, waits for them, and re-layouts  1.77 us (2%)
    pallas_call x1, Pallas kernels, on_device(): pl.pallas_call(kernel, out_shape=jax.ShapeDtypeStruct((tokens, width), bf...  77.2 us
    unnamed x1, local copies, waits for them, and re-layouts  1.77 us

profile of v4, /device:TPU:1, one launch (start us, length us, event | category | flops | bytes accessed | tf_op | source)
XLA Modules:
  0.0 79.0 jit_solution(18264753353120507998)
XLA Ops:
  0.0 77.2 %moe_down_combine.1 = bf16[256,768]{1,0:T(8,128)(2,1)} custom-call(bf16[1,16,96,1408]{3,2,1,0:T(8,128)(2,1)} %hidden.1, bf16[1,1408,3072]{2,1,0:T(8,128)(2,1)} %weight.1, s32[4,256]{1,0:T(4,128)} %bitcast.2, f32[4,256]{1,0:T(4,128)} %bitcast.3, bf16[256,768]{1,0:T(8,128)(2,1)} %residual.1), custom_call_target="tpu_custom_call" | custom-call | tf_op jit(solution)/shard_map/moe_down_combine/pallas_call | solution.py:464
  77.2 1.8 %copy.7 = bf16[256,768]{1,0:T(8,128)(2,1)} copy(bf16[256,768]{1,0:T(8,128)(2,1)} %moe_down_combine.1) | data formatting | bytes 786432

commit v5 on v4

--- a/solution.py
+++ b/solution.py
@@ -17,13 +17,15 @@
 SETS = ((1, -1), (1, 0), (2, 0), (3, 0), (4, 0), (5, 0), (6, 0), (7, 0), (2, 1), (3, -1), (4, 1))
 
 ORDER = (
-    1, 2, 3, 8, 9, 16, 17, 18, 19, 10, 11, 128, 72, 80, 136, 384, 385, 144,
-    521, 531, 210, 386, 200, 129, 24, 88, 32, 137, 96, 33, 538, 145, 219, 217, 544, 227,
-    225, 34, 387, 25, 40, 226, 104, 41, 42, 43, 160, 26, 554, 27, 458, 450, 216, 235,
-    35, 48, 49, 50, 152, 51, 233, 466, 112, 168, 56, 120, 57, 560, 243, 242, 161, 241,
-    58, 59, 176, 533, 524, 153, 169, 232, 184, 267, 482, 548, 177, 258, 474, 257, 540, 221,
-    490, 256, 320, 229, 185, 498, 556, 321, 564, 237, 245, 506, 322, 576, 576,
+    16, 8, 9, 72, 17, 80, 384, 2, 128, 385, 521, 32, 531, 33, 200, 10, 24, 88,
+    136, 386, 210, 96, 129, 537, 48, 49, 547, 40, 219, 18, 25, 41, 3, 224, 144, 42,
+    26, 216, 225, 218, 50, 34, 160, 450, 152, 226, 112, 387, 168, 104, 555, 137, 145, 27,
+    560, 11, 243, 233, 153, 232, 19, 176, 161, 43, 241, 242, 458, 56, 466, 120, 234, 524,
+    474, 35, 57, 267, 169, 541, 257, 177, 533, 256, 51, 258, 320, 482, 548, 220, 58, 490,
+    229, 184, 557, 498, 321, 564, 236, 185, 245, 322, 59, 506,
 )
+FIRST_LOADS = ((False, (0, 2)), (True, (0, 1)), (False, (1, 3)), (True, (2, 3)))
+ROW_ORDER = [code // 8 for code in ORDER if code < 64 and code % 8 == 0]
 WORDS = tuple(
     sum(code << 10 * j for j, code in enumerate(ORDER[t : t + 3])) for t in range(0, len(ORDER), 3)
 )
@@ -32,8 +34,8 @@
 def kernel(
     hidden, weight, routes, scores, residual, out,
     w_early, w_late, h_buf, part, ring_in, blocks, hand_b, hand_a, raw_in, tok, tok_in, late, late_in,
-    all_routes, all_scores, counts, table, upright, pick_hi, pick_lo,
-    we_sem, wl_sem, h_sem, ring_send, ring_recv, hb_send, hb_recv, ha_send, ha_recv, raw_send, raw_recv,
+    all_routes, all_scores, rest, staged, counts, table, upright, pick_hi, pick_lo,
+    we_sem, wl_sem, h_sem, own_sem, out_sem, ring_send, ring_recv, hb_send, hb_recv, ha_send, ha_recv, raw_send, raw_recv,
     tok_send, tok_recv, late_send, late_recv, route_send, route_recv, score_send, score_recv,
 ):
     expert, tp = lax.axis_index("expert"), lax.axis_index("tp")
@@ -77,13 +79,24 @@
 
     for other in range(2):
         h_load(0, other).start()
-    for r in range(n_tp):
-        w_load(r, False).start()
-    for r in range(n_tp):
-        w_load(r, True).start()
-    for i in range(1, CHIPS):
+    for early, rs in FIRST_LOADS:
+        for r in rs:
+            w_load(r, early).start()
+    for i in ROW_ORDER:
         for other in range(2):
             h_load(i, other).start()
+
+    own_copies = [
+        pltpu.make_async_copy(routes, all_routes.at[LAST], own_sem.at[0]),
+        pltpu.make_async_copy(scores, all_scores.at[LAST], own_sem.at[1]),
+        pltpu.make_async_copy(residual, rest, own_sem.at[2]),
+    ]
+    for copy in own_copies:
+        copy.start()
+
+    def out_copy(j):
+        at = pl.ds(j * STREAM, STREAM)
+        return pltpu.make_async_copy(staged.at[:, at], out.at[:, at], out_sem.at[j])
 
     def route_copies(i):
         peer = {"expert": 2 * chip(-ahead(i)) + core}
@@ -192,10 +205,10 @@
         part[pl.ds(2 * i, 2), r] = product.astype(bf16).reshape(2, cap, TP_FIRST)
 
     def matmul_early(i, r):
-        for way in range(n_tp - 1):
-            @pl.when((i == 0) & (r == way + 1))
+        for new in (2, 3):
+            @pl.when((i == 0) & (r == new))
             def _():
-                w_load(way + 1, True).wait()
+                w_load(new, True).wait()
 
         @pl.when(r == 0)
         def _():
@@ -325,6 +338,8 @@
         for j in range(1, LAST):
             for copy in route_copies(j):
                 copy.wait_recv()
+        for copy in own_copies[:2]:
+            copy.wait()
         for j, (group, shift) in enumerate(SETS):
             chosen, value = all_routes[group], all_scores[group]
             share = value / jnp.sum(value, axis=0, keepdims=True)
@@ -369,20 +384,29 @@
         nothing,
     )
 
+    def first_late(r):
+        w_load(r, False).wait()
+        at = slice(r * STREAM, (r + 1) * STREAM)
+        product = jnp.dot(left_rows(0), w_late[:, at], preferred_element_type=f32).astype(bf16)
+        blocks[0, r, 0] = product[:cap]
+        hand_b[0, r] = product[cap:]
+
     await_rows(0)
-    for r in range(n_tp):
-        w_load(r, False).wait()
-    product_late(0)
-    w_load(0, True).wait()
-    product_early(0, 0)
+    first_late(0)
     pl.semaphore_wait(barrier, 2 + len(greeted))
     for i in range(1, LAST):
         for copy in route_copies(i):
             copy.start()
-    raw_start(0, range(n_tp))
-    ring_copy(0, 0, 0).start()
-    all_routes[LAST] = routes[...]
-    all_scores[LAST] = scores[...]
+    raw_start(0, (0,))
+    first_late(2)
+    raw_start(0, (2,))
+    for way in range(2):
+        w_load(way, True).wait()
+        product_early(0, way)
+        ring_copy(0, way, 0).start()
+    for r in (1, 3):
+        first_late(r)
+        raw_start(0, (r,))
 
     def steps(j, carry):
         word = jnp.int32(WORDS[0])
@@ -407,16 +431,21 @@
 
     lax.fori_loop(0, len(WORDS), steps, 0)
 
+    own_copies[2].wait()
     for way in range(2):
         late_copy(way, n_tp - 2).wait_recv()
         here = slice(way * half, (way + 1) * half)
         mixed = late[n_tp - 1, here].astype(f32) + late_in[n_tp - 2, way].astype(f32)
-        out[here, TP_FIRST:] = (residual[here, TP_FIRST:].astype(f32) + mixed).astype(bf16)
+        staged[here, TP_FIRST:] = (rest[here, TP_FIRST:].astype(f32) + mixed).astype(bf16)
+    out_copy(n_early).start()
     hand_copy(LAST, True).wait_recv()
-    totals = [weighted(LAST, n_tp + h) for h in range(n_early)]
+    totals = []
     for h in range(n_early):
         at = slice(h * STREAM, (h + 1) * STREAM)
-        out[:, at] = (residual[:, at].astype(f32) + chain_end(n_tp + h, totals[h])).astype(bf16)
+        totals.append(rest[:, at].astype(f32) + weighted(LAST, n_tp + h))
+    for h in range(n_early):
+        staged[:, h * STREAM : (h + 1) * STREAM] = chain_end(n_tp + h, totals[h]).astype(bf16)
+        out_copy(h).start()
 
     def drain(i, carry):
         for hop in range(n_tp - 1):
@@ -438,6 +467,8 @@
         return carry
 
     lax.fori_loop(0, CHIPS, drain, 0)
+    for j in range(n_early + 1):
+        out_copy(j).wait()
     for stage in range(2):
         for s in range(blocks.shape[1]):
             for other in range(2):
@@ -459,13 +490,12 @@
     streams = n_tp + early
     bf16, f32 = jnp.bfloat16, jnp.float32
     any_space = pl.BlockSpec(memory_space=pl.ANY)
-    vmem = pl.BlockSpec(memory_space=pltpu.VMEM)
     dma = pltpu.SemaphoreType.DMA
     return pl.pallas_call(
         kernel,
         out_shape=jax.ShapeDtypeStruct((tokens, width), bf16),
-        in_specs=[any_space, any_space, vmem, vmem, vmem],
-        out_specs=vmem,
+        in_specs=[any_space] * 5,
+        out_specs=any_space,
         scratch_shapes=[
             pltpu.VMEM((n_tp, units, TP_FIRST), bf16),
             pltpu.VMEM((units, n_tp * STREAM), bf16),
@@ -482,6 +512,8 @@
             pltpu.VMEM((n_tp - 1, 2, tokens // 2, STREAM), bf16),
             pltpu.VMEM((CHIPS, top, tokens), jnp.int32),
             pltpu.VMEM((CHIPS, top, tokens), f32),
+            pltpu.VMEM((tokens, width), bf16),
+            pltpu.VMEM((tokens, width), bf16),
             pltpu.VMEM((32, tokens), f32),
             pltpu.VMEM((128, tokens), f32),
             pltpu.VMEM((tokens, 128), f32),
@@ -490,6 +522,8 @@
             dma((n_tp,)),
             dma((n_tp,)),
             dma((sources,)),
+            dma((3,)),
+            dma((early + 1,)),
             dma((n_tp - 1, sources)),
             dma((n_tp - 1, sources)),
             dma((CHIPS,)),

time: 79.4 us -> 76 us (0.957)
  Pallas kernels: 77.2 us -> 74.1 us
    pallas_call x1, Pallas kernels: 77.2 us -> 74.1 us  [on_device(): pl.pallas_call(kernel, out_shape=jax.ShapeDtypeStruct((tokens, width), bf...]
where the time goes in v5:
time: 76 us; the launch traced here: 75.9 us
  Pallas kernels  74.1 us (97%)
  local copies, waits for them, and re-layouts  1.77 us (2%)
    pallas_call x1, Pallas kernels, on_device(): pl.pallas_call(kernel, out_shape=jax.ShapeDtypeStruct((tokens, width), bf...  74.1 us
    unnamed x1, local copies, waits for them, and re-layouts  1.77 us

profile of v5, /device:TPU:1, one launch (start us, length us, event | category | flops | bytes accessed | tf_op | source)
XLA Modules:
  0.0 75.9 jit_solution(9860127502986210197)
XLA Ops:
  0.0 74.1 %moe_down_combine.1 = bf16[256,768]{1,0:T(8,128)(2,1)} custom-call(bf16[1,16,96,1408]{3,2,1,0:T(8,128)(2,1)} %hidden.1, bf16[1,1408,3072]{2,1,0:T(8,128)(2,1)} %weight.1, s32[4,256]{1,0:T(4,128)} %bitcast.2, f32[4,256]{1,0:T(4,128)} %bitcast.3, bf16[256,768]{1,0:T(8,128)(2,1)} %residual.1), custom_call_target="tpu_custom_call" | custom-call | tf_op jit(solution)/shard_map/moe_down_combine/pallas_call | solution.py:494
  74.1 1.8 %copy.7 = bf16[256,768]{1,0:T(8,128)(2,1)} copy(bf16[256,768]{1,0:T(8,128)(2,1)} %moe_down_combine.1) | data formatting | bytes 786432

commit v6 on v5

--- a/solution.py
+++ b/solution.py
@@ -17,12 +17,12 @@
 SETS = ((1, -1), (1, 0), (2, 0), (3, 0), (4, 0), (5, 0), (6, 0), (7, 0), (2, 1), (3, -1), (4, 1))
 
 ORDER = (
-    16, 8, 9, 72, 17, 80, 384, 2, 128, 385, 521, 32, 531, 33, 200, 10, 24, 88,
-    136, 386, 210, 96, 129, 537, 48, 49, 547, 40, 219, 18, 25, 41, 3, 224, 144, 42,
-    26, 216, 225, 218, 50, 34, 160, 450, 152, 226, 112, 387, 168, 104, 555, 137, 145, 27,
-    560, 11, 243, 233, 153, 232, 19, 176, 161, 43, 241, 242, 458, 56, 466, 120, 234, 524,
-    474, 35, 57, 267, 169, 541, 257, 177, 533, 256, 51, 258, 320, 482, 548, 220, 58, 490,
-    229, 184, 557, 498, 321, 564, 236, 185, 245, 322, 59, 506,
+    16, 2, 17, 8, 72, 9, 80, 128, 24, 384, 385, 25, 10, 520, 531, 88, 136, 32,
+    210, 96, 201, 129, 386, 545, 539, 218, 33, 18, 227, 144, 40, 3, 387, 41, 48, 217,
+    34, 226, 216, 104, 160, 112, 137, 42, 224, 26, 49, 554, 450, 235, 152, 11, 35, 168,
+    233, 562, 27, 243, 240, 50, 145, 153, 458, 176, 161, 232, 241, 169, 56, 524, 57, 120,
+    19, 267, 474, 466, 533, 541, 177, 258, 482, 257, 51, 256, 320, 58, 548, 43, 220, 490,
+    59, 184, 229, 498, 557, 321, 564, 185, 236, 245, 322, 506,
 )
 FIRST_LOADS = ((False, (0, 2)), (True, (0, 1)), (False, (1, 3)), (True, (2, 3)))
 ROW_ORDER = [code // 8 for code in ORDER if code < 64 and code % 8 == 0]
@@ -34,8 +34,8 @@
 def kernel(
     hidden, weight, routes, scores, residual, out,
     w_early, w_late, h_buf, part, ring_in, blocks, hand_b, hand_a, raw_in, tok, tok_in, late, late_in,
-    all_routes, all_scores, rest, staged, counts, table, upright, pick_hi, pick_lo,
-    we_sem, wl_sem, h_sem, own_sem, out_sem, ring_send, ring_recv, hb_send, hb_recv, ha_send, ha_recv, raw_send, raw_recv,
+    all_routes, all_scores, rest, counts, table, upright, pick_hi, pick_lo,
+    we_sem, wl_sem, h_sem, own_sem, ring_send, ring_recv, hb_send, hb_recv, ha_send, ha_recv, raw_send, raw_recv,
     tok_send, tok_recv, late_send, late_recv, route_send, route_recv, score_send, score_recv,
 ):
     expert, tp = lax.axis_index("expert"), lax.axis_index("tp")
@@ -55,14 +55,6 @@
     def ahead(i):
         return (CHIPS // 2 - (i + 1) // 2) * (1 if i % 2 == 1 else -1)
 
-    barrier = pltpu.get_barrier_semaphore()
-    for peer in (up, down):
-        pl.semaphore_signal(barrier, inc=1, device_id={"tp": peer}, device_id_type=MESH)
-    greeted = [2 * chip(-ahead(i)) + core for i in range(1, LAST)]
-    greeted += [partner, 2 * chip(1) + 1 - core, 2 * chip(-1) + 1 - core]
-    for peer in greeted:
-        pl.semaphore_signal(barrier, inc=1, device_id={"expert": peer}, device_id_type=MESH)
-
     def w_load(r, early):
         start = lax.rem(tp + SLICE_SHIFT[r], n_tp) * width
         if early:
@@ -79,7 +71,19 @@
 
     for other in range(2):
         h_load(0, other).start()
-    for early, rs in FIRST_LOADS:
+    early, rs = FIRST_LOADS[0]
+    for r in rs:
+        w_load(r, early).start()
+
+    barrier = pltpu.get_barrier_semaphore()
+    for peer in (up, down):
+        pl.semaphore_signal(barrier, inc=1, device_id={"tp": peer}, device_id_type=MESH)
+    greeted = [2 * chip(-ahead(i)) + core for i in range(1, LAST)]
+    greeted += [partner, 2 * chip(1) + 1 - core, 2 * chip(-1) + 1 - core]
+    for peer in greeted:
+        pl.semaphore_signal(barrier, inc=1, device_id={"expert": peer}, device_id_type=MESH)
+
+    for early, rs in FIRST_LOADS[1:]:
         for r in rs:
             w_load(r, early).start()
     for i in ROW_ORDER:
@@ -93,10 +97,6 @@
     ]
     for copy in own_copies:
         copy.start()
-
-    def out_copy(j):
-        at = pl.ds(j * STREAM, STREAM)
-        return pltpu.make_async_copy(staged.at[:, at], out.at[:, at], out_sem.at[j])
 
     def route_copies(i):
         peer = {"expert": 2 * chip(-ahead(i)) + core}
@@ -436,16 +436,14 @@
         late_copy(way, n_tp - 2).wait_recv()
         here = slice(way * half, (way + 1) * half)
         mixed = late[n_tp - 1, here].astype(f32) + late_in[n_tp - 2, way].astype(f32)
-        staged[here, TP_FIRST:] = (rest[here, TP_FIRST:].astype(f32) + mixed).astype(bf16)
-    out_copy(n_early).start()
+        out[here, TP_FIRST:] = (rest[here, TP_FIRST:].astype(f32) + mixed).astype(bf16)
     hand_copy(LAST, True).wait_recv()
     totals = []
     for h in range(n_early):
         at = slice(h * STREAM, (h + 1) * STREAM)
         totals.append(rest[:, at].astype(f32) + weighted(LAST, n_tp + h))
     for h in range(n_early):
-        staged[:, h * STREAM : (h + 1) * STREAM] = chain_end(n_tp + h, totals[h]).astype(bf16)
-        out_copy(h).start()
+        out[:, h * STREAM : (h + 1) * STREAM] = chain_end(n_tp + h, totals[h]).astype(bf16)
 
     def drain(i, carry):
         for hop in range(n_tp - 1):
@@ -467,8 +465,6 @@
         return carry
 
     lax.fori_loop(0, CHIPS, drain, 0)
-    for j in range(n_early + 1):
-        out_copy(j).wait()
     for stage in range(2):
         for s in range(blocks.shape[1]):
             for other in range(2):
@@ -493,9 +489,9 @@
     dma = pltpu.SemaphoreType.DMA
     return pl.pallas_call(
         kernel,
-        out_shape=jax.ShapeDtypeStruct((tokens, width), bf16),
+        out_shape=pltpu.VMEM((tokens, width), bf16),
         in_specs=[any_space] * 5,
-        out_specs=any_space,
+        out_specs=pl.BlockSpec(memory_space=pltpu.VMEM),
         scratch_shapes=[
             pltpu.VMEM((n_tp, units, TP_FIRST), bf16),
             pltpu.VMEM((units, n_tp * STREAM), bf16),
@@ -513,7 +509,6 @@
             pltpu.VMEM((CHIPS, top, tokens), jnp.int32),
             pltpu.VMEM((CHIPS, top, tokens), f32),
             pltpu.VMEM((tokens, width), bf16),
-            pltpu.VMEM((tokens, width), bf16),
             pltpu.VMEM((32, tokens), f32),
             pltpu.VMEM((128, tokens), f32),
             pltpu.VMEM((tokens, 128), f32),
@@ -523,7 +518,6 @@
             dma((n_tp,)),
             dma((sources,)),
             dma((3,)),
-            dma((early + 1,)),
             dma((n_tp - 1, sources)),
             dma((n_tp - 1, sources)),
             dma((CHIPS,)),
@@ -542,7 +536,7 @@
             dma((LAST,)),
         ],
         compiler_params=pltpu.CompilerParams(
-            collective_id=0, has_side_effects=True, vmem_limit_bytes=60 * 1024 * 1024
+            collective_id=0, has_side_effects=True, vmem_limit_bytes=56 * 1024 * 1024
         ),
         name="moe_down_combine",
     )(hidden, down_weight, routes.T, route_weight.T, residual)

time: 76 us -> 73.8 us (0.971)
  Pallas kernels: 74.1 us -> 73 us
  local copies, waits for them, and re-layouts: 1.77 us -> 0.75 us
    pallas_call x1, Pallas kernels: 74.1 us -> 73 us  [on_device(): pl.pallas_call(kernel, out_shape=pltpu.VMEM((tokens, width), bf16), in_sp...]
    unnamed x1, local copies, waits for them, and re-layouts: 1.77 us -> 0.75 us
where the time goes in v6:
time: 73.8 us; the launch traced here: 73.7 us
  Pallas kernels  73 us (99%)
  local copies, waits for them, and re-layouts  0.75 us (1%)
    pallas_call x1, Pallas kernels, on_device(): pl.pallas_call(kernel, out_shape=pltpu.VMEM((tokens, width), bf16), in_sp...  73 us

profile of v6, /device:TPU:1, one launch (start us, length us, event | category | flops | bytes accessed | tf_op | source)
XLA Modules:
  0.0 73.7 jit_solution(7860511656227283965)
XLA Ops:
  0.0 73.0 %moe_down_combine.1 = bf16[256,768]{1,0:T(8,128)(2,1)S(1)} custom-call(bf16[1,16,96,1408]{3,2,1,0:T(8,128)(2,1)} %hidden.1, bf16[1,1408,3072]{2,1,0:T(8,128)(2,1)} %weight.1, s32[4,256]{1,0:T(4,128)} %bitcast.2, f32[4,256]{1,0:T(4,128)} %bitcast.3, bf16[256,768]{1,0:T(8,128)(2,1)} %residual.1), custom_call_target="tpu_custom_call" | custom-call | tf_op jit(solution)/shard_map/moe_down_combine/pallas_call | solution.py:490
  73.0 0.7 %copy.7 = bf16[256,768]{1,0:T(8,128)(2,1)} copy(bf16[256,768]{1,0:T(8,128)(2,1)S(1)} %moe_down_combine.1) | data formatting | bytes 786432

commit v7 on v6

--- a/solution.py
+++ b/solution.py
@@ -17,12 +17,12 @@
 SETS = ((1, -1), (1, 0), (2, 0), (3, 0), (4, 0), (5, 0), (6, 0), (7, 0), (2, 1), (3, -1), (4, 1))
 
 ORDER = (
-    16, 2, 17, 8, 72, 9, 80, 128, 24, 384, 385, 25, 10, 520, 531, 88, 136, 32,
-    210, 96, 201, 129, 386, 545, 539, 218, 33, 18, 227, 144, 40, 3, 387, 41, 48, 217,
-    34, 226, 216, 104, 160, 112, 137, 42, 224, 26, 49, 554, 450, 235, 152, 11, 35, 168,
-    233, 562, 27, 243, 240, 50, 145, 153, 458, 176, 161, 232, 241, 169, 56, 524, 57, 120,
-    19, 267, 474, 466, 533, 541, 177, 258, 482, 257, 51, 256, 320, 58, 548, 43, 220, 490,
-    59, 184, 229, 498, 557, 321, 564, 185, 236, 245, 322, 506,
+    8, 16, 17, 72, 9, 80, 2, 128, 384, 385, 521, 24, 25, 200, 531, 88, 10, 136,
+    32, 210, 96, 33, 386, 537, 544, 129, 18, 225, 34, 40, 219, 144, 48, 3, 216, 227,
+    137, 387, 11, 112, 160, 218, 41, 226, 26, 104, 145, 450, 560, 152, 553, 35, 232, 19,
+    49, 234, 50, 243, 242, 42, 241, 235, 168, 27, 458, 161, 153, 466, 176, 56, 120, 524,
+    169, 266, 482, 57, 533, 256, 474, 259, 257, 541, 177, 51, 320, 548, 58, 43, 220, 490,
+    229, 184, 498, 557, 321, 564, 236, 185, 245, 322, 59, 506,
 )
 FIRST_LOADS = ((False, (0, 2)), (True, (0, 1)), (False, (1, 3)), (True, (2, 3)))
 ROW_ORDER = [code // 8 for code in ORDER if code < 64 and code % 8 == 0]

time: 73.8 us -> 73.4 us (level)
  no operation moved by 1% of the time
where the time goes in v7:
time: 73.4 us; the launch traced here: 73.3 us
  Pallas kernels  72.5 us (99%)
  local copies, waits for them, and re-layouts  0.75 us (1%)
    pallas_call x1, Pallas kernels, on_device(): pl.pallas_call(kernel, out_shape=pltpu.VMEM((tokens, width), bf16), in_sp...  72.5 us

profile of v7, /device:TPU:1, one launch (start us, length us, event | category | flops | bytes accessed | tf_op | source)
XLA Modules:
  0.0 73.3 jit_solution(10582866630895117526)
XLA Ops:
  0.0 72.5 %moe_down_combine.1 = bf16[256,768]{1,0:T(8,128)(2,1)S(1)} custom-call(bf16[1,16,96,1408]{3,2,1,0:T(8,128)(2,1)} %hidden.1, bf16[1,1408,3072]{2,1,0:T(8,128)(2,1)} %weight.1, s32[4,256]{1,0:T(4,128)} %bitcast.2, f32[4,256]{1,0:T(4,128)} %bitcast.3, bf16[256,768]{1,0:T(8,128)(2,1)} %residual.1), custom_call_target="tpu_custom_call" | custom-call | tf_op jit(solution)/shard_map/moe_down_combine/pallas_call | solution.py:490
  72.5 0.7 %copy.7 = bf16[256,768]{1,0:T(8,128)(2,1)} copy(bf16[256,768]{1,0:T(8,128)(2,1)S(1)} %moe_down_combine.1) | data formatting | bytes 786432

commit v8 on v7

--- a/solution.py
+++ b/solution.py
@@ -431,6 +431,39 @@
 
     lax.fori_loop(0, len(WORDS), steps, 0)
 
+    def settle_blocks(i, carry):
+        for hop in range(n_tp - 1):
+            for way in range(2):
+                ring_copy(i, way, hop).wait_send()
+
+        @pl.when(i > 0)
+        def _():
+            for early in (False, True):
+                hand_copy(i, early).wait_send()
+
+        return carry
+
+    def settle_sums(i, carry):
+        for s in range(blocks.shape[1]):
+            @pl.when(i != (2 if goes_up(s) else 1))
+            def _():
+                tok_copy(i, s, z).wait_send()
+
+        return carry
+
+    lax.fori_loop(0, LAST, settle_blocks, 0)
+    lax.fori_loop(1, LAST - 2, settle_sums, 0)
+    for stage in range(2):
+        for s in range(blocks.shape[1]):
+            for other in range(2):
+                raw_copy(stage, s, other).wait_send()
+    for i in range(1, LAST):
+        for copy in route_copies(i):
+            copy.wait_send()
+    for hop in range(n_tp - 2):
+        for way in range(2):
+            late_copy(way, hop).wait_send()
+
     own_copies[2].wait()
     for way in range(2):
         late_copy(way, n_tp - 2).wait_recv()
@@ -445,36 +478,12 @@
     for h in range(n_early):
         out[:, h * STREAM : (h + 1) * STREAM] = chain_end(n_tp + h, totals[h]).astype(bf16)
 
-    def drain(i, carry):
-        for hop in range(n_tp - 1):
-            for way in range(2):
-                ring_copy(i, way, hop).wait_send()
-
-        @pl.when(i > 0)
-        def _():
-            for early in (False, True):
-                hand_copy(i, early).wait_send()
-
-        @pl.when((i > 0) & (i < LAST))
-        def _():
-            for s in range(blocks.shape[1]):
-                @pl.when(i != (2 if goes_up(s) else 1))
-                def _():
-                    tok_copy(i, s, z).wait_send()
-
-        return carry
-
-    lax.fori_loop(0, CHIPS, drain, 0)
-    for stage in range(2):
-        for s in range(blocks.shape[1]):
-            for other in range(2):
-                raw_copy(stage, s, other).wait_send()
-    for i in range(1, LAST):
-        for copy in route_copies(i):
-            copy.wait_send()
-    for hop in range(n_tp - 1):
-        for way in range(2):
-            late_copy(way, hop).wait_send()
+    for s in range(blocks.shape[1]):
+        for i in (LAST - 2, LAST - 1):
+            tok_copy(i, s, z).wait_send()
+    settle_blocks(jnp.int32(LAST), 0)
+    for way in range(2):
+        late_copy(way, n_tp - 2).wait_send()
 
 
 def on_device(hidden, down_weight, routes, route_weight, residual):

time: 73.4 us -> 73.1 us (level)
  no operation moved by 1% of the time
where the time goes in v8:
time: 73.1 us
  Pallas kernels  72.3 us (99%)
  local copies, waits for them, and re-layouts  0.75 us (1%)
    pallas_call x1, Pallas kernels, on_device(): pl.pallas_call(kernel, out_shape=pltpu.VMEM((tokens, width), bf16), in_sp...  72.3 us

profile of v8, /device:TPU:1, one launch (start us, length us, event | category | flops | bytes accessed | tf_op | source)
XLA Modules:
  0.0 73.1 jit_solution(6094109985960265057)
XLA Ops:
  0.0 72.3 %moe_down_combine.1 = bf16[256,768]{1,0:T(8,128)(2,1)S(1)} custom-call(bf16[1,16,96,1408]{3,2,1,0:T(8,128)(2,1)} %hidden.1, bf16[1,1408,3072]{2,1,0:T(8,128)(2,1)} %weight.1, s32[4,256]{1,0:T(4,128)} %bitcast.2, f32[4,256]{1,0:T(4,128)} %bitcast.3, bf16[256,768]{1,0:T(8,128)(2,1)} %residual.1), custom_call_target="tpu_custom_call" | custom-call | tf_op jit(solution)/shard_map/moe_down_combine/pallas_call | solution.py:499
  72.3 0.7 %copy.7 = bf16[256,768]{1,0:T(8,128)(2,1)} copy(bf16[256,768]{1,0:T(8,128)(2,1)S(1)} %moe_down_combine.1) | data formatting | bytes 786432

commit v9 on v7

--- a/solution.py
+++ b/solution.py
@@ -432,16 +432,16 @@
     lax.fori_loop(0, len(WORDS), steps, 0)
 
     own_copies[2].wait()
+    hand_copy(LAST, True).wait_recv()
+    totals = []
+    for h in range(n_early):
+        at = slice(h * STREAM, (h + 1) * STREAM)
+        totals.append(rest[:, at].astype(f32) + weighted(LAST, n_tp + h))
     for way in range(2):
         late_copy(way, n_tp - 2).wait_recv()
         here = slice(way * half, (way + 1) * half)
         mixed = late[n_tp - 1, here].astype(f32) + late_in[n_tp - 2, way].astype(f32)
         out[here, TP_FIRST:] = (rest[here, TP_FIRST:].astype(f32) + mixed).astype(bf16)
-    hand_copy(LAST, True).wait_recv()
-    totals = []
-    for h in range(n_early):
-        at = slice(h * STREAM, (h + 1) * STREAM)
-        totals.append(rest[:, at].astype(f32) + weighted(LAST, n_tp + h))
     for h in range(n_early):
         out[:, h * STREAM : (h + 1) * STREAM] = chain_end(n_tp + h, totals[h]).astype(bf16)
 

time: 73.4 us -> 73.4 us (level)
  no operation moved by 1% of the time
where the time goes in v9:
time: 73.4 us; the launch traced here: 73.3 us
  Pallas kernels  72.6 us (99%)
  local copies, waits for them, and re-layouts  0.75 us (1%)
    pallas_call x1, Pallas kernels, on_device(): pl.pallas_call(kernel, out_shape=pltpu.VMEM((tokens, width), bf16), in_sp...  72.6 us

profile of v9, /device:TPU:1, one launch (start us, length us, event | category | flops | bytes accessed | tf_op | source)
XLA Modules:
  0.0 73.3 jit_solution(8521116933098376633)
XLA Ops:
  0.0 72.6 %moe_down_combine.1 = bf16[256,768]{1,0:T(8,128)(2,1)S(1)} custom-call(bf16[1,16,96,1408]{3,2,1,0:T(8,128)(2,1)} %hidden.1, bf16[1,1408,3072]{2,1,0:T(8,128)(2,1)} %weight.1, s32[4,256]{1,0:T(4,128)} %bitcast.2, f32[4,256]{1,0:T(4,128)} %bitcast.3, bf16[256,768]{1,0:T(8,128)(2,1)} %residual.1), custom_call_target="tpu_custom_call" | custom-call | tf_op jit(solution)/shard_map/moe_down_combine/pallas_call | solution.py:490
  72.6 0.7 %copy.7 = bf16[256,768]{1,0:T(8,128)(2,1)} copy(bf16[256,768]{1,0:T(8,128)(2,1)S(1)} %moe_down_combine.1) | data formatting | bytes 786432
